TPU v7x, 512 devices: a whole 4x8x8 slice. The times are simulated.
512 devices in a mesh: mode: 8 (over x, z_lo), space: 64 (over y, z_hi, core).
Axes of the slice: x: 4, y: 8, z: 8 (z_hi: 4, z_lo: 2; z = z_hi * 2 + z_lo), core: 2. Of those that a mesh axis runs over, the one named last changes fastest.
Arguments:
- mode_fields: bfloat16 [512, 2, 256, 256], P('mode', None, 'space'), may hold values from -6 to 6
- metric: float32 [3, 256, 256], P(None, 'space'), may hold values from 0.5 to 2
- plan: int32 [4, 2], replicated, may hold values from 0 to 7, as said below
Outputs:
- tensor: float32 [4096, 512], P('space', 'mode')
Inputs may be any that keep to these rules, and one draw needn't show every extreme that they name: `plan`: rows 0 and 1 name the advecting blocks, rows 2 and 3 the advected blocks: column 0 a mode group, column 1 a half of its modes (0 or 1). Blocks may repeat.
All inputs are finite; a program needn't handle non-finite values.
Results may differ from a plain program's by a relative error of at most 0.0041.
Values may be sent and summed in bfloat16 or wider, within the bound.
No kernel may reach another device: no remote copies, remote signals or barrier semaphores. Data moves between devices by JAX's collectives and lax.ppermute only.
A program may use at most 64 MiB of HBM per device.

v0:
```python
import jax
import jax.numpy as jnp
from jax import lax
from jax.sharding import PartitionSpec as P


def broadcast(block, axis, holder):
    block = jnp.where(lax.axis_index(axis) == holder, block, jnp.zeros_like(block))
    return lax.psum(block, axis)


def with_halo(block, sides, width):
    for axis, dim in sides:
        count = lax.axis_size(axis)
        forward = [(i, i + 1) for i in range(count - 1)]
        backward = [(target, source) for source, target in forward]
        low = lax.ppermute(
            lax.slice_in_dim(block, block.shape[dim] - width, None, axis=dim), axis, forward
        )
        high = lax.ppermute(lax.slice_in_dim(block, 0, width, axis=dim), axis, backward)
        block = jnp.concatenate([low, block, high], axis=dim)
    return block


def stencil(padded, metric):
    widened = padded.astype(jnp.float32)
    along_x = (widened[:, :, 2:, :] - widened[:, :, :-2, :]) * metric[0]
    interior = jnp.pad(widened[:, :, 1:-1, :], ((0, 0), (0, 0), (0, 0), (1, 1)))
    along_y = (interior[:, :, :, 2:] - interior[:, :, :, :-2]) * metric[1]
    return jnp.stack((along_x, along_y), axis=1).astype(jnp.bfloat16)


def advect(column, slopes, weight):
    widened = column.astype(jnp.float32)
    mixed = widened[0] * slopes[:, 0].astype(jnp.float32) + widened[1] * slopes[:, 1].astype(
        jnp.float32
    )
    return (mixed * weight).astype(jnp.bfloat16).reshape(slopes.shape[0], -1)


def body(mode_fields, metric, plan):
    half_size = mode_fields.shape[0] // 2

    def own_block(source_row):
        return lax.dynamic_slice_in_dim(mode_fields, plan[source_row, 1] * half_size, half_size, 0)

    pieces = [
        broadcast(own_block(source_row), "mode", plan[source_row, 0]) for source_row in range(2)
    ]
    movers = jnp.concatenate(pieces, axis=0)
    shipped = []
    for source_row in range(2, 4):
        padded = with_halo(own_block(source_row), (("space", 2),), 1)
        shipped.append(broadcast(stencil(padded, metric), "mode", plan[source_row, 0]))
    slopes = jnp.concatenate(shipped, axis=0)
    test_rows = mode_fields.reshape(mode_fields.shape[0], -1)
    advected_count = slopes.shape[0]
    norm_factor = float(mode_fields.shape[2] * lax.axis_size("space") * mode_fields.shape[3]) ** (
        -0.5
    )

    def project(column):
        advected_field = advect(column, slopes, metric[2])
        return lax.dot_general(
            advected_field, test_rows, (((1,), (1,)), ((), ())), preferred_element_type=jnp.float32
        )

    slot_rows = movers.shape[0] * advected_count // lax.axis_size("space")
    mover_count = slot_rows * lax.axis_size("space") // advected_count
    blocks = lax.map(project, movers, batch_size=min(mover_count, 4))
    return lax.psum_scatter(
        blocks.reshape(slot_rows * lax.axis_size("space"), test_rows.shape[0]) * norm_factor,
        "space",
        scatter_dimension=0,
        tiled=True,
    )


def solution(mesh):
    return jax.shard_map(
        body,
        mesh=mesh,
        in_specs=(P("mode", None, "space", None), P(None, "space", None), P()),
        out_specs=P("space", "mode"),
        check_vma=False,
    )
```

profile of v0, /device:TPU:1, one launch (start us, length us, event | category | flops | bytes accessed | tf_op | source)
XLA Modules:
  0.0 331.2 jit_solution(9886116430528512822)
XLA Ops:
  6.5 1.7 fusion.21
  9.5 1.4 constant_dynamic-slice_fusion.4
  10.8 7.2 %collective-permute-start = (bf16[32,2,1,256]{3,2,1,0:T(2,128)(2,1)S(1)}, bf16[32,2,1,256]{3,2,1,0:T(2,128)(2,1)S(1)}, u32[]{:S(2)}, u32[]{:S(2)}) collective-permute-start(bf16[32,2,1,256]{3,2,1,0:T(2,128)(2,1)S(1)} %get-tuple-element.68), channel_id=1, source_target_pairs={{0,1},{1,2},{2,3},{3,4},{4,5},{5,6},{6,7},{7,8},{8,9},{9,10},{10,1... | collective-permute-start | bytes 98312 | tf_op jit(solution)/shard_map/ppermute | solution.py:17
  18.0 2.9 collective-permute-start.1
  20.9 3.6 %collective-permute-start.2 = (bf16[32,2,1,256]{3,2,1,0:T(2,128)(2,1)S(1)}, bf16[32,2,1,256]{3,2,1,0:T(2,128)(2,1)S(1)}, u32[]{:S(2)}, u32[]{:S(2)}) collective-permute-start(bf16[32,2,1,256]{3,2,1,0:T(2,128)(2,1)S(1)} %get-tuple-element.70), channel_id=1, source_target_pairs={{0,1},{1,2},{2,3},{3,4},{4,5},{5,6},{6,7},{7,8},{8,9},{9,10},{10,1... | collective-permute-start | bytes 98312 | tf_op jit(solution)/shard_map/ppermute | solution.py:17
  24.5 1.9 collective-permute-start.3
  29.0 0.7 slice_bitcast_fusion.4
  29.7 2.0 constant_dynamic-slice_fusion.6
  33.7 0.6 fusion.20
  34.3 1.2 maximum_select_fusion
  35.8 89.2 %all-reduce.5.cloned.1.call-done = (bf16[32,2,4,256]{3,2,1,0:T(4,128)(2,1)}, bf16[32,2,4,256]{3,2,1,0:T(4,128)(2,1)}, bf16[32,2,2,4,256]{4,3,2,0,1:T(4,128)(2,1)}, bf16[32,2,2,4,256]{4,3,2,0,1:T(4,128)(2,1)}) async-done(((bf16[32,2,4,256]{3,2,1,0:T(4,128)(2,1)}, bf16[32,2,4,256]{3,2,1,0:T(4,128)(2,1)}, bf16[32,2,2,4,256]{4,3,2,0,1:T(4,128)(2,1)}, bf16[32,2,2,4,256]{4,3,2,0,1:T(4,128)(2,1)}), ...) | async-done | bytes 786448 | tf_op jit(solution)/shard_map/psum | solution.py:9
  124.9 1.4 pad_maximum_fusion
  126.3 1.1 pad_maximum_fusion.1
  127.5 42.4 %while.10 = (s32[]{:T(128)}, f32[16,4,64,64]{3,2,1,0:T(8,128)}, bf16[16,4,2,4,256]{4,3,2,1,0:T(4,128)(2,1)S(1)}, bf16[64,2,2,4,256]{4,3,2,0,1:T(4,128)(2,1)S(1)}...) while((s32[]{:T(128)}, f32[16,4,64,64]{3,2,1,0:T(8,128)}, ...), condition=%wide.region_5.6_spmd, body=%wide.region_4.5_spmd.sunk | while | flops 70000640 | bytes 5567057 | solution.py:70
  128.3 0.7 slice_bitcast_fusion.7
  129.0 1.1 fusion.27
  131.0 0.7 slice_bitcast_fusion.7
  131.7 1.1 fusion.27
  133.6 0.7 slice_bitcast_fusion.7
  134.3 1.1 fusion.27
  136.2 0.7 slice_bitcast_fusion.7
  136.9 1.1 fusion.27
  138.9 0.7 slice_bitcast_fusion.7
  139.6 1.1 fusion.27
  141.5 0.7 slice_bitcast_fusion.7
  142.2 1.1 fusion.27
  144.2 0.7 slice_bitcast_fusion.7
  144.9 1.1 fusion.27
  146.8 0.7 slice_bitcast_fusion.7
  147.5 1.1 fusion.27
  149.5 0.7 slice_bitcast_fusion.7
  150.2 1.1 fusion.27
  152.1 0.7 slice_bitcast_fusion.7
  152.8 1.1 fusion.27
  154.8 0.7 slice_bitcast_fusion.7
  155.5 1.1 fusion.27
  157.4 0.7 slice_bitcast_fusion.7
  158.1 1.1 fusion.27
  160.1 0.7 slice_bitcast_fusion.7
  160.8 1.1 fusion.27
  162.7 0.7 slice_bitcast_fusion.7
  163.4 1.1 fusion.27
  165.4 0.7 slice_bitcast_fusion.7
  166.1 1.1 fusion.27
  168.0 0.7 slice_bitcast_fusion.7
  168.7 1.1 fusion.27
  169.8 3.2 broadcast_multiply_fusion
  173.1 151.2 %reduce-scatter.2.cloned.1.call-done = f32[64,64]{1,0:T(8,128)} async-done(((f32[4096,64]{1,0:T(8,128)}), f32[64,64]{1,0:T(8,128)}) %reduce-scatter.2.cloned.1.call-update) | async-done | bytes 16400 | tf_op jit(solution)/shard_map/reduce_scatter | solution.py:71
  (191 shorter events, 13.5 us)
Async XLA Ops:
  6.5 118.4 %all-reduce.5.cloned.1.call-start = ((), (), s32[]{:S(2)}) async-start(), calls=%async_computation.2 | async-start | bytes 1572864 | tf_op jit(solution)/shard_map/psum | solution.py:9
  10.8 22.1 %collective-permute-start = (bf16[32,2,1,256]{3,2,1,0:T(2,128)(2,1)S(1)}, bf16[32,2,1,256]{3,2,1,0:T(2,128)(2,1)S(1)}, u32[]{:S(2)}, u32[]{:S(2)}) collective-permute-start(bf16[32,2,1,256]{3,2,1,0:T(2,128)(2,1)S(1)} %get-tuple-element.68), channel_id=1, source_target_pairs={{0,1},{1,2},{2,3},{3,4},{4,5},{5,6},{6,7},{7,8},{8,9},{9,10},{10,1... | collective-permute-start | bytes 98312 | tf_op jit(solution)/shard_map/ppermute | solution.py:17
  18.0 14.9 %collective-permute-start.1 = (bf16[32,2,1,256]{3,2,1,0:T(2,128)(2,1)S(1)}, bf16[32,2,1,256]{3,2,1,0:T(2,128)(2,1)S(1)}, u32[]{:S(2)}, u32[]{:S(2)}) collective-permute-start(bf16[32,2,1,256]{3,2,1,0:T(2,128)(2,1)S(1)} %get-tuple-element.71), channel_id=1, source_target_pairs={{1,0},{2,1},{3,2},{4,3},{5,4},{6,5},{7,6},{8,7},{9,8},{10,9},{11,1... | collective-permute-start | bytes 98312 | tf_op jit(solution)/shard_map/ppermute | solution.py:20
  20.9 12.2 %collective-permute-start.2 = (bf16[32,2,1,256]{3,2,1,0:T(2,128)(2,1)S(1)}, bf16[32,2,1,256]{3,2,1,0:T(2,128)(2,1)S(1)}, u32[]{:S(2)}, u32[]{:S(2)}) collective-permute-start(bf16[32,2,1,256]{3,2,1,0:T(2,128)(2,1)S(1)} %get-tuple-element.70), channel_id=1, source_target_pairs={{0,1},{1,2},{2,3},{3,4},{4,5},{5,6},{6,7},{7,8},{8,9},{9,10},{10,1... | collective-permute-start | bytes 98312 | tf_op jit(solution)/shard_map/ppermute | solution.py:17
  24.5 8.6 %collective-permute-start.3 = (bf16[32,2,1,256]{3,2,1,0:T(2,128)(2,1)S(1)}, bf16[32,2,1,256]{3,2,1,0:T(2,128)(2,1)S(1)}, u32[]{:S(2)}, u32[]{:S(2)}) collective-permute-start(bf16[32,2,1,256]{3,2,1,0:T(2,128)(2,1)S(1)} %get-tuple-element.69), channel_id=1, source_target_pairs={{1,0},{2,1},{3,2},{4,3},{5,4},{6,5},{7,6},{8,7},{9,8},{10,9},{11,1... | collective-permute-start | bytes 98312 | tf_op jit(solution)/shard_map/ppermute | solution.py:20
  33.4 2.2 copy-start
  35.5 288.8 %reduce-scatter.2.cloned.1.call-start = ((), (), s32[]{:S(2)}) async-start(), calls=%async_computation.1 | async-start | bytes 2129920 | tf_op jit(solution)/shard_map/reduce_scatter | solution.py:71
Sparse Core Ops, SparseCore 0:
  35.6 89.2 all-reduce.4
  173.2 151.0 reduce-scatter.1
where the time goes:
time: 336 us; the launch traced here: 331 us
  waiting for transfers between devices  240 us (71%)
  local copies, waits for them, and re-layouts  25.2 us (8%)
  between operations  18.5 us (6%)
  matrix products  18 us (5%)
  starting transfers between devices  15.6 us (5%)
  other arithmetic  12.6 us (4%)
    reduce_scatter x1, waiting for transfers between devices, body(): lax.psum_scatter(blocks.reshape(slot_rows * lax.axis_size('space'), test_...  151 us
    psum x1, waiting for transfers between devices, broadcast(): return lax.psum(block, axis)  89.2 us
    dot_general x16, matrix products, project(): lax.dot_general(advected_field, test_rows, (((1,), (1,)), ((), ())), pref...  18 us
    mul x16, local copies, waits for them, and re-layouts, advect(): return (mixed * weight).astype(jnp.bfloat16).reshape(slopes.shape[0], -1)  11.1 us
    ppermute x2, starting transfers between devices, with_halo(): lax.ppermute(lax.slice_in_dim(block, block.shape[dim] - width, None, axis...  10.8 us
  transfers between devices with their start and end apart: 6, of which 2 were waited for; matrix products, arithmetic and copies ran while one was open for 1% of the time, Pallas kernels for 0%

commit v1 on v0

v1 whole, which is shorter than its diff:
```python
import jax
import jax.numpy as jnp
from jax import lax
from jax.experimental import pallas as pl
from jax.experimental.pallas import tpu as pltpu
from jax.sharding import Mesh, PartitionSpec as P

MODE = ("x", "zl")
SPACE = ("y", "zh", "c")
JB = 8


def kernel(c_ref, metric_ref, recv_ref, test_ref, out_ref, s_ref, wm_ref, phi_ref, f_ref, *, send):
    groups = recv_ref.shape[0]
    n = groups * recv_ref.shape[2]
    ny = recv_ref.shape[3]
    f32 = jnp.float32

    def row(index):
        return recv_ref[:, index].astype(f32).reshape(n, ny)

    @pl.when(pl.program_id(0) == 0)
    def _():
        lane = lax.broadcasted_iota(jnp.int32, (n, ny), 1)
        for c in range(2):
            for r in range(4):
                low = row(16 + c) if r == 0 else row(8 + 4 * c + r - 1)
                high = row(18 + c) if r == 3 else row(8 + 4 * c + r + 1)
                mid = row(8 + 4 * c + r)
                along_x = (high - low) * metric_ref[0, pl.ds(r, 1), :]
                after = jnp.where(lane == ny - 1, 0.0, pltpu.roll(mid, ny - 1, 1))
                before = jnp.where(lane == 0, 0.0, pltpu.roll(mid, 1, 1))
                along_y = (after - before) * metric_ref[1, pl.ds(r, 1), :]
                s_ref[0, 4 * c + r] = along_x.astype(jnp.bfloat16).astype(f32)
                s_ref[1, 4 * c + r] = along_y.astype(jnp.bfloat16).astype(f32)
                wm_ref[4 * c + r] = row(4 * c + r) * metric_ref[2, pl.ds(r, 1), :]
                phi_ref[:, pl.ds((4 * c + r) * ny, ny)] = test_ref[:, 4 * c + r].reshape(n, ny)

    parity = 1 - c_ref[0] if send else c_ref[0]
    base = pl.program_id(0) * (2 * JB) + parity
    for cr in range(8):
        r = cr % 4
        s0 = s_ref[0, cr]
        s1 = s_ref[1, cr]
        for b in range(JB):
            j = base + 2 * b
            field = wm_ref[r, pl.ds(j, 1), :] * s0 + wm_ref[4 + r, pl.ds(j, 1), :] * s1
            f_ref[pl.ds(b * n, n), pl.ds(cr * ny, ny)] = field.astype(jnp.bfloat16)
    res = lax.dot_general(f_ref[...], phi_ref[...], (((1,), (1,)), ((), ())), preferred_element_type=f32)
    res = res.reshape(JB, n, n)
    out_ref[...] = jnp.concatenate([res[:, : n // 2], res[:, n // 2 :]], axis=2)


def project(core, metric, recv, test, send):
    groups, _, m, ny = recv.shape
    n = groups * m
    movers = n // 2
    return pl.pallas_call(
        lambda *refs: kernel(*refs, send=send),
        grid=(movers // JB,),
        in_specs=[
            pl.BlockSpec(memory_space=pltpu.SMEM),
            pl.BlockSpec(metric.shape, lambda i: (0, 0, 0)),
            pl.BlockSpec(recv.shape, lambda i: (0, 0, 0, 0)),
            pl.BlockSpec(test.shape, lambda i: (0, 0, 0, 0)),
        ],
        out_specs=pl.BlockSpec((JB, n // 2, 2 * n), lambda i: (i, 0, 0)),
        out_shape=jax.ShapeDtypeStruct((movers, n // 2, 2 * n), jnp.float32),
        scratch_shapes=[
            pltpu.VMEM((2, 8, n, ny), jnp.float32),
            pltpu.VMEM((8, n, ny), jnp.float32),
            pltpu.VMEM((n, 8 * ny), jnp.bfloat16),
            pltpu.VMEM((JB * n, 8 * ny), jnp.bfloat16),
        ],
        compiler_params=pltpu.CompilerParams(dimension_semantics=("arbitrary",)),
        name="project_send" if send else "project_keep",
    )(core, metric, recv, test)


def body(mode_fields, metric, plan):
    n = mode_fields.shape[0]
    ny = mode_fields.shape[3]
    groups = lax.axis_size(MODE)
    m = n // groups
    half = groups // 2
    fields = mode_fields.reshape(groups, m, 2, 4, ny).transpose(0, 2, 3, 1, 4).reshape(groups, 8, m, ny)

    def candidates(row):
        return lax.dynamic_slice_in_dim(fields, plan[row, 1] * half, half, 0)

    movers = jnp.concatenate([candidates(0), candidates(1)], axis=0)
    carried = jnp.concatenate([candidates(2), candidates(3)], axis=0)
    pieces = lax.all_to_all(
        jnp.concatenate([movers, carried], axis=1), MODE, 0, 0, tiled=True
    )
    block = lax.axis_index(MODE) // half
    mover = lax.dynamic_index_in_dim(pieces[:, :8], plan[block, 0], 0, keepdims=False)
    moved = lax.dynamic_index_in_dim(pieces[:, 8:], plan[2 + block, 0], 0, keepdims=False)
    count = lax.axis_size(SPACE)
    forward = [(i, i + 1) for i in range(count - 1)]
    backward = [(i + 1, i) for i in range(count - 1)]
    by_row = moved.reshape(2, 4, m, ny)
    low = lax.ppermute(by_row[:, 3], SPACE, forward)
    high = lax.ppermute(by_row[:, 0], SPACE, backward)
    piece = jnp.concatenate([mover, moved, low, high], axis=0)
    recv = lax.all_to_all(
        jnp.broadcast_to(piece[None], (groups,) + piece.shape), MODE, 0, 0, tiled=True
    )
    core = lax.axis_index("c").astype(jnp.int32).reshape(1)
    sent = project(core, metric, recv, fields, True)
    other = lax.ppermute(sent, "c", [(0, 1), (1, 0)])
    kept = project(core, metric, recv, fields, False)
    shares = lax.all_to_all(kept + other, ("y", "zh"), 0, 0, tiled=True)
    norm_factor = float(4 * count * ny) ** (-0.5)
    total = jnp.sum(shares, axis=0) * norm_factor
    return jnp.concatenate([total[:, :n], total[:, n:]], axis=0)


def solution(mesh):
    fine = Mesh(mesh.devices.reshape(4, 2, 8, 4, 2), ("x", "zl", "y", "zh", "c"))
    return jax.shard_map(
        body,
        mesh=fine,
        in_specs=(P(MODE, None, SPACE, None), P(None, SPACE, None), P()),
        out_specs=P(SPACE, MODE),
        check_vma=False,
    )
```

time: 336 us -> 99.7 us (0.30)
  waiting for transfers between devices: 240 us -> 17 us
  blocking collectives: 0 us -> 32.9 us
  local copies, waits for them, and re-layouts: 25.2 us -> 4.89 us
  matrix products: 18 us -> 0 us
  between operations: 18.5 us -> 6.48 us
  Pallas kernels: 0 us -> 10.6 us
  other arithmetic: 12.6 us -> 2.66 us
  starting transfers between devices: 15.6 us -> 23.2 us
    reduce_scatter x1 -> x0, waiting for transfers between devices: 151 us -> none  [body(): lax.psum_scatter(blocks.reshape(slot_rows * lax.axis_size('space'), test_...]
    psum x1 -> x0, waiting for transfers between devices: 89.2 us -> none  [broadcast(): return lax.psum(block, axis)]
    all_to_all x0 -> x1, blocking collectives: none -> 32.9 us  [body(): shares = lax.all_to_all(kept + other, ('y', 'zh'), 0, 0, tiled=True)]
    dot_general x16 -> x0, matrix products: 18 us -> none  [project(): lax.dot_general(advected_field, test_rows, (((1,), (1,)), ((), ())), pref...]
    all_to_all x0 -> x2, waiting for transfers between devices: none -> 13.1 us  [the longest x1 9.36 us: body(): lax.all_to_all(jnp.broadcast_to(piece[None], (groups,) + piece.shape), MO...]
    mul x97 -> x0, local copies, waits for them, and re-layouts: 13 us -> none  [the longest x16 11.1 us: advect(): return (mixed * weight).astype(jnp.bfloat16).reshape(slopes.shape[0], -1)]
    pallas_call x0 -> x2, Pallas kernels: none -> 10.6 us  [project(): pl.pallas_call(lambda *refs: kernel(*refs, send=send), grid=(movers // JB...]
    all_to_all x0 -> x2, starting transfers between devices: none -> 10.2 us  [the longest x1 6.65 us: body(): lax.all_to_all(jnp.concatenate([movers, carried], axis=1), MODE, 0, 0, ti...]
  transfers between devices with their start and end apart: 6 -> 5, of which waited for: 2 -> 3; matrix products, arithmetic and copies ran while one was open for 1% -> 0% of each run, Pallas kernels for 0% -> 5%
where the time goes in v1:
time: 99.7 us; the launch traced here: 97.7 us
  blocking collectives  32.9 us (33%)
  starting transfers between devices  23.2 us (23%)
  waiting for transfers between devices  17 us (17%)
  Pallas kernels  10.6 us (11%)
  between operations  6.48 us (6%)
  local copies, waits for them, and re-layouts  4.89 us (5%)
  other arithmetic  2.66 us (3%)
    all_to_all x1, blocking collectives, body(): shares = lax.all_to_all(kept + other, ('y', 'zh'), 0, 0, tiled=True)  32.9 us
    pallas_call x2, Pallas kernels, project(): pl.pallas_call(lambda *refs: kernel(*refs, send=send), grid=(movers // JB...  10.6 us
    all_to_all x1, waiting for transfers between devices, body(): lax.all_to_all(jnp.broadcast_to(piece[None], (groups,) + piece.shape), MO...  9.36 us
    ppermute x1, starting transfers between devices, body(): low = lax.ppermute(by_row[:, 3], SPACE, forward)  9.19 us
    all_to_all x1, starting transfers between devices, body(): lax.all_to_all(jnp.concatenate([movers, carried], axis=1), MODE, 0, 0, ti...  6.65 us
    ppermute x1, waiting for transfers between devices, body(): high = lax.ppermute(by_row[:, 0], SPACE, backward)  3.91 us
    all_to_all x1, waiting for transfers between devices, body(): lax.all_to_all(jnp.concatenate([movers, carried], axis=1), MODE, 0, 0, ti...  3.74 us
    all_to_all x1, starting transfers between devices, body(): lax.all_to_all(jnp.broadcast_to(piece[None], (groups,) + piece.shape), MO...  3.54 us
  transfers between devices with their start and end apart: 5, of which 3 were waited for; matrix products, arithmetic and copies ran while one was open for 0% of the time, Pallas kernels for 5%

profile of v1, /device:TPU:1, one launch (start us, length us, event | category | flops | bytes accessed | tf_op | source)
XLA Modules:
  0.0 97.7 jit_solution(9481546313921242531)
XLA Ops:
  0.0 0.0 copy-start.2
  0.0 0.7 copy-done.2
  0.7 0.7 constant_dynamic-slice_fusion.2
  3.9 1.0 %copy.5 = bf16[8,8,2,4,256]{4,1,3,2,0:T(8,128)(2,1)S(1)} copy(bf16[8,8,2,4,256]{4,3,2,1,0:T(4,128)(2,1)} %bitcast.23) | data formatting | bytes 524288 | tf_op jit(solution)/shard_map/reshape | solution.py:86
  4.9 0.0 copy-start
  5.0 0.6 copy-done
  5.6 0.9 maximum_maximum_fusion
  6.4 6.6 %all-to-all-start = ((bf16[8,16,8,256]{3,2,1,0:T(8,128)(2,1)}), bf16[8,16,8,256]{3,2,1,0:T(8,128)(2,1)S(1)}, u32[]{:S(2)}, u32[]{:S(2)}) async-start(bf16[8,16,8,256]{3,2,1,0:T(8,128)(2,1)} %maximum_maximum_fusion), calls=%async_computation | async-start | bytes 1048576 | tf_op jit(solution)/shard_map/all_to_all | solution.py:93
  16.9 3.7 %all-to-all-done = bf16[8,16,8,256]{3,2,1,0:T(8,128)(2,1)S(1)} async-done(((bf16[8,16,8,256]{3,2,1,0:T(8,128)(2,1)}), bf16[8,16,8,256]{3,2,1,0:T(8,128)(2,1)S(1)}, u32[]{:S(2)}, u32[]{:S(2)}) %all-to-all-start) | async-done | bytes 524320 | tf_op jit(solution)/shard_map/all_to_all | solution.py:93
  20.7 9.2 %collective-permute-start = (bf16[2,8,256]{2,1,0:T(8,128)(2,1)S(1)}, bf16[2,8,256]{2,1,0:T(8,128)(2,1)S(1)}, u32[]{:S(2)}, u32[]{:S(2)}) collective-permute-start(bf16[2,8,256]{2,1,0:T(8,128)(2,1)S(1)} %get-tuple-element.11), channel_id=1, source_target_pairs={{0,1},{1,2},{2,3},{3,4},{4,5},{5,6},{6,7},{7,8},{8,9},{9,10},{10,1... | collective-permute-start | bytes 24584 | tf_op jit(solution)/shard_map/ppermute | solution.py:103
  29.9 1.9 %collective-permute-start.1 = (bf16[2,8,256]{2,1,0:T(8,128)(2,1)S(1)}, bf16[2,8,256]{2,1,0:T(8,128)(2,1)S(1)}, u32[]{:S(2)}, u32[]{:S(2)}) collective-permute-start(bf16[2,8,256]{2,1,0:T(8,128)(2,1)S(1)} %get-tuple-element.12), channel_id=1, source_target_pairs={{1,0},{2,1},{3,2},{4,3},{5,4},{6,5},{7,6},{8,7},{9,8},{10,9},{11,1... | collective-permute-start | bytes 24584 | tf_op jit(solution)/shard_map/ppermute | solution.py:104
  31.9 0.0 collective-permute-done
  31.9 3.9 %collective-permute-done.1 = bf16[2,8,256]{2,1,0:T(8,128)(2,1)S(1)} collective-permute-done((bf16[2,8,256]{2,1,0:T(8,128)(2,1)S(1)}, bf16[2,8,256]{2,1,0:T(8,128)(2,1)S(1)}, u32[]{:S(2)}, u32[]{:S(2)}) %collective-permute-start.1) | collective-permute-done | bytes 8224 | tf_op jit(solution)/shard_map/ppermute | solution.py:104
  35.8 0.9 broadcast_in_dim.2
  36.7 3.5 %all-to-all-start.1 = ((bf16[8,20,8,256]{3,2,1,0:T(8,128)(2,1)}), bf16[8,20,8,256]{3,2,1,0:T(8,128)(2,1)S(1)}, u32[]{:S(2)}, u32[]{:S(2)}) async-start(bf16[8,20,8,256]{3,2,1,0:T(8,128)(2,1)} %broadcast_in_dim.2), calls=%async_computation.1 | async-start | bytes 1310720 | tf_op jit(solution)/shard_map/all_to_all | solution.py:106
  40.2 9.4 %all-to-all-done.1.refs_2_ = bf16[8,20,8,256]{3,2,1,0:T(8,128)(2,1)S(1)} async-done(((bf16[8,20,8,256]{3,2,1,0:T(8,128)(2,1)}), bf16[8,20,8,256]{3,2,1,0:T(8,128)(2,1)S(1)}, u32[]{:S(2)}, u32[]{:S(2)}) %all-to-all-start.1) | async-done | bytes 655392 | tf_op jit(solution)/shard_map/all_to_all | solution.py:106
  49.6 0.0 copy-start.1
  49.6 0.8 copy-done.1
  50.4 5.3 %project_send.1 = f32[32,32,128]{2,1,0:T(8,128)} custom-call(s32[1]{0:T(128)} %bitcast.refs_0_, f32[3,4,256]{2,1,0:T(4,128)} %refs_1_.3, bf16[8,20,8,256]{3,2,1,0:T(8,128)(2,1)} %copy-done.1, bf16[8,8,8,256]{3,2,1,0:T(8,128)(2,1)} %bitcast.21), custom_call_target="tpu_custom_call" | custom-call | tf_op jit(solution)/shard_map/project_send/pallas_call | solution.py:58
  55.7 1.9 %collective-permute-start.2 = (f32[32,32,128]{2,1,0:T(8,128)}, f32[32,32,128]{2,1,0:T(8,128)S(1)}, u32[]{:S(2)}, u32[]{:S(2)}) collective-permute-start(f32[32,32,128]{2,1,0:T(8,128)} %project_send.1), channel_id=1, source_target_pairs={{0,1},{1,0},{2,3},{3,2},{4,5},{5,4},{6,7},{7,6},{8,9},{9,8},{10,11... | collective-permute-start | bytes 1572872 | tf_op jit(solution)/shard_map/ppermute | solution.py:111
  57.6 5.3 %project_keep.1 = f32[32,32,128]{2,1,0:T(8,128)} custom-call(s32[1]{0:T(128)} %bitcast.refs_0_, f32[3,4,256]{2,1,0:T(4,128)} %refs_1_.3, bf16[8,20,8,256]{3,2,1,0:T(8,128)(2,1)} %copy-done.1, bf16[8,8,8,256]{3,2,1,0:T(8,128)(2,1)} %bitcast.22), custom_call_target="tpu_custom_call" | custom-call | tf_op jit(solution)/shard_map/project_keep/pallas_call | solution.py:58
  63.0 0.0 collective-permute-done.2
  63.0 1.1 %add.47 = f32[32,32,128]{2,1,0:T(8,128)S(1)} add(f32[32,32,128]{2,1,0:T(8,128)} %project_keep.1, f32[32,32,128]{2,1,0:T(8,128)S(1)} %collective-permute-done.2) | non-fusion elementwise | flops 131072 | bytes 1572864 | tf_op jit(solution)/shard_map/add | solution.py:113
  64.1 32.9 %all_to_all.15 = f32[32,32,128]{2,1,0:T(8,128)S(1)} all-to-all(f32[32,32,128]{2,1,0:T(8,128)S(1)} %add.47), channel_id=1, replica_groups=mesh['x'=4,'zl'=2,'y'=8,'zh'=4,'c'=2] {'y','zh'}, dimensions={0} | all-to-all | bytes 1048576 | tf_op jit(solution)/shard_map/all_to_all | solution.py:113
  97.0 0.1 fusion.1
  97.1 0.6 pad_maximum_fusion.1
  (9 shorter events, 0.2 us)
Async XLA Ops:
  0.0 0.7 copy-start.2
  4.9 0.7 copy-start
  6.4 14.2 %all-to-all-start = ((bf16[8,16,8,256]{3,2,1,0:T(8,128)(2,1)}), bf16[8,16,8,256]{3,2,1,0:T(8,128)(2,1)S(1)}, u32[]{:S(2)}, u32[]{:S(2)}) async-start(bf16[8,16,8,256]{3,2,1,0:T(8,128)(2,1)} %maximum_maximum_fusion), calls=%async_computation | async-start | bytes 1048576 | tf_op jit(solution)/shard_map/all_to_all | solution.py:93
  20.7 11.2 %collective-permute-start = (bf16[2,8,256]{2,1,0:T(8,128)(2,1)S(1)}, bf16[2,8,256]{2,1,0:T(8,128)(2,1)S(1)}, u32[]{:S(2)}, u32[]{:S(2)}) collective-permute-start(bf16[2,8,256]{2,1,0:T(8,128)(2,1)S(1)} %get-tuple-element.11), channel_id=1, source_target_pairs={{0,1},{1,2},{2,3},{3,4},{4,5},{5,6},{6,7},{7,8},{8,9},{9,10},{10,1... | collective-permute-start | bytes 24584 | tf_op jit(solution)/shard_map/ppermute | solution.py:103
  29.9 5.9 %collective-permute-start.1 = (bf16[2,8,256]{2,1,0:T(8,128)(2,1)S(1)}, bf16[2,8,256]{2,1,0:T(8,128)(2,1)S(1)}, u32[]{:S(2)}, u32[]{:S(2)}) collective-permute-start(bf16[2,8,256]{2,1,0:T(8,128)(2,1)S(1)} %get-tuple-element.12), channel_id=1, source_target_pairs={{1,0},{2,1},{3,2},{4,3},{5,4},{6,5},{7,6},{8,7},{9,8},{10,9},{11,1... | collective-permute-start | bytes 24584 | tf_op jit(solution)/shard_map/ppermute | solution.py:104
  36.7 12.9 %all-to-all-start.1 = ((bf16[8,20,8,256]{3,2,1,0:T(8,128)(2,1)}), bf16[8,20,8,256]{3,2,1,0:T(8,128)(2,1)S(1)}, u32[]{:S(2)}, u32[]{:S(2)}) async-start(bf16[8,20,8,256]{3,2,1,0:T(8,128)(2,1)} %broadcast_in_dim.2), calls=%async_computation.1 | async-start | bytes 1310720 | tf_op jit(solution)/shard_map/all_to_all | solution.py:106
  49.6 0.8 copy-start.1
  55.7 7.2 %collective-permute-start.2 = (f32[32,32,128]{2,1,0:T(8,128)}, f32[32,32,128]{2,1,0:T(8,128)S(1)}, u32[]{:S(2)}, u32[]{:S(2)}) collective-permute-start(f32[32,32,128]{2,1,0:T(8,128)} %project_send.1), channel_id=1, source_target_pairs={{0,1},{1,0},{2,3},{3,2},{4,5},{5,4},{6,7},{7,6},{8,9},{9,8},{10,11... | collective-permute-start | bytes 1572872 | tf_op jit(solution)/shard_map/ppermute | solution.py:111

commit v2 on v1

v2 whole, which is shorter than its diff:
```python
import jax
import jax.numpy as jnp
from jax import lax
from jax.experimental import pallas as pl
from jax.experimental.pallas import tpu as pltpu
from jax.sharding import Mesh, PartitionSpec as P

MODE = ("x", "zl")
SPACE = ("y", "zh", "c")
JB = 8
CHUNKS = 2
LIMIT = 16 * 2**20
SMEM = pl.BlockSpec(memory_space=pltpu.SMEM)
ANY = pl.BlockSpec(memory_space=pl.ANY)


def run_copies(pairs, sems):
    copies = [pltpu.make_async_copy(src, dst, sems.at[i]) for i, (src, dst) in enumerate(pairs)]
    for copy in copies:
        copy.start()
    for copy in copies:
        copy.wait()


def pack_kernel(plan_ref, fields_ref, low_ref, high_ref, out_ref, sems):
    half = fields_ref.shape[0] // 2
    pairs = []
    for b in range(2):
        here = pl.ds(b * half, half)
        mover = pl.ds(plan_ref[b, 1] * half, half)
        moved = pl.ds(plan_ref[2 + b, 1] * half, half)
        pairs += [
            (fields_ref.at[mover], out_ref.at[here, 0:8]),
            (fields_ref.at[moved], out_ref.at[here, 8:16]),
            (low_ref.at[moved], out_ref.at[here, 16:18]),
            (high_ref.at[moved], out_ref.at[here, 18:20]),
        ]
    run_copies(pairs, sems)


def pack(plan, fields, low, high):
    groups, _, m, ny = fields.shape
    return pl.pallas_call(
        pack_kernel,
        in_specs=[SMEM, ANY, ANY, ANY],
        out_specs=ANY,
        out_shape=jax.ShapeDtypeStruct((groups, 20, m, ny), fields.dtype),
        scratch_shapes=[pltpu.SemaphoreType.DMA((8,))],
        compiler_params=pltpu.CompilerParams(vmem_limit_bytes=LIMIT),
        name="pack",
    )(plan, fields, low, high)


def choose_kernel(plan_ref, place_ref, pieces_ref, out_ref, sems):
    groups = pieces_ref.shape[0]
    block = place_ref[0] // (groups // 2)
    mover = plan_ref[block, 0]
    moved = plan_ref[2 + block, 0]
    pairs = []
    for g in range(groups):
        pairs += [
            (pieces_ref.at[mover, 0:8], out_ref.at[g, 0:8]),
            (pieces_ref.at[moved, 8:20], out_ref.at[g, 8:20]),
        ]
    run_copies(pairs, sems)


def choose(plan, place, pieces):
    return pl.pallas_call(
        choose_kernel,
        in_specs=[SMEM, SMEM, ANY],
        out_specs=ANY,
        out_shape=jax.ShapeDtypeStruct(pieces.shape, pieces.dtype),
        scratch_shapes=[pltpu.SemaphoreType.DMA((16,))],
        compiler_params=pltpu.CompilerParams(vmem_limit_bytes=LIMIT),
        name="choose",
    )(plan, place, pieces)


def kernel(
    c_ref, metric_any, recv_any, test_any, out_ref,
    metric_ref, recv_ref, test_ref, s_ref, wm_ref, phi_ref, f_ref, sems, *, send, chunk
):
    groups, _, m, ny = recv_ref.shape
    n = groups * m
    part = groups // CHUNKS
    k = n // CHUNKS
    f32 = jnp.float32

    def row(index):
        return recv_ref[chunk * part : (chunk + 1) * part, index].astype(f32).reshape(k, ny)

    @pl.when(pl.program_id(0) == 0)
    def _():
        run_copies([(metric_any, metric_ref), (recv_any, recv_ref), (test_any, test_ref)], sems)
        lane = lax.broadcasted_iota(jnp.int32, (k, ny), 1)
        for c in range(2):
            for r in range(4):
                low = row(16 + c) if r == 0 else row(8 + 4 * c + r - 1)
                high = row(18 + c) if r == 3 else row(8 + 4 * c + r + 1)
                mid = row(8 + 4 * c + r)
                along_x = (high - low) * metric_ref[0, pl.ds(r, 1), :]
                after = jnp.where(lane == ny - 1, 0.0, pltpu.roll(mid, ny - 1, 1))
                before = jnp.where(lane == 0, 0.0, pltpu.roll(mid, 1, 1))
                along_y = (after - before) * metric_ref[1, pl.ds(r, 1), :]
                s_ref[0, 4 * c + r] = along_x.astype(jnp.bfloat16).astype(f32)
                s_ref[1, 4 * c + r] = along_y.astype(jnp.bfloat16).astype(f32)
                mover = recv_ref[:, 4 * c + r].astype(f32).reshape(n, ny)
                wm_ref[4 * c + r] = mover * metric_ref[2, pl.ds(r, 1), :]
                phi_ref[:, pl.ds((4 * c + r) * ny, ny)] = test_ref[:, 4 * c + r].reshape(n, ny)

    parity = 1 - c_ref[0] if send else c_ref[0]
    base = pl.program_id(0) * (2 * JB) + parity
    for cr in range(8):
        r = cr % 4
        s0 = s_ref[0, cr]
        s1 = s_ref[1, cr]
        for b in range(JB):
            j = base + 2 * b
            field = wm_ref[r, pl.ds(j, 1), :] * s0 + wm_ref[4 + r, pl.ds(j, 1), :] * s1
            f_ref[pl.ds(b * k, k), pl.ds(cr * ny, ny)] = field.astype(jnp.bfloat16)
    res = lax.dot_general(f_ref[...], phi_ref[...], (((1,), (1,)), ((), ())), preferred_element_type=f32)
    res = res.reshape(JB, k, n)
    out_ref[...] = jnp.concatenate([res[:, : k // 2], res[:, k // 2 :]], axis=2)


def project(core, metric, recv, test, send, chunk):
    groups, _, m, ny = recv.shape
    n = groups * m
    movers = n // 2
    k = n // CHUNKS
    return pl.pallas_call(
        lambda *refs: kernel(*refs, send=send, chunk=chunk),
        grid=(movers // JB,),
        in_specs=[SMEM, ANY, ANY, ANY],
        out_specs=pl.BlockSpec((JB, k // 2, 2 * n), lambda i: (i, 0, 0)),
        out_shape=jax.ShapeDtypeStruct((movers, k // 2, 2 * n), jnp.float32),
        scratch_shapes=[
            pltpu.VMEM(metric.shape, metric.dtype),
            pltpu.VMEM(recv.shape, recv.dtype),
            pltpu.VMEM(test.shape, test.dtype),
            pltpu.VMEM((2, 8, k, ny), jnp.float32),
            pltpu.VMEM((8, n, ny), jnp.float32),
            pltpu.VMEM((n, 8 * ny), jnp.bfloat16),
            pltpu.VMEM((JB * k, 8 * ny), jnp.bfloat16),
            pltpu.SemaphoreType.DMA((3,)),
        ],
        compiler_params=pltpu.CompilerParams(dimension_semantics=("arbitrary",), vmem_limit_bytes=LIMIT),
        name=f"project_{chunk}_{'send' if send else 'keep'}",
    )(core, metric, recv, test)


def body(mode_fields, metric, plan):
    n = mode_fields.shape[0]
    ny = mode_fields.shape[3]
    groups = lax.axis_size(MODE)
    m = n // groups
    by_row = mode_fields.reshape(groups, m, 2, 4, ny).transpose(0, 2, 3, 1, 4)
    fields = by_row.reshape(groups, 8, m, ny)
    count = lax.axis_size(SPACE)
    forward = [(i, i + 1) for i in range(count - 1)]
    backward = [(i + 1, i) for i in range(count - 1)]
    low = lax.ppermute(by_row[:, :, 3], SPACE, forward)
    high = lax.ppermute(by_row[:, :, 0], SPACE, backward)
    pieces = lax.all_to_all(pack(plan, fields, low, high), MODE, 0, 0, tiled=True)
    place = lax.axis_index(MODE).astype(jnp.int32).reshape(1)
    recv = lax.all_to_all(choose(plan, place, pieces), MODE, 0, 0, tiled=True)
    core = lax.axis_index("c").astype(jnp.int32).reshape(1)
    norm_factor = float(4 * count * ny) ** (-0.5)
    shares = []
    for chunk in range(CHUNKS):
        sent = project(core, metric, recv, fields, True, chunk)
        other = lax.ppermute(sent, "c", [(0, 1), (1, 0)])
        kept = project(core, metric, recv, fields, False, chunk)
        shares.append(lax.all_to_all(kept + other, ("y", "zh"), 0, 0, tiled=True))
    rows = []
    for share in shares:
        total = jnp.sum(share, axis=0) * norm_factor
        rows += [total[:, :n], total[:, n:]]
    return jnp.concatenate(rows, axis=0)


def solution(mesh):
    fine = Mesh(mesh.devices.reshape(4, 2, 8, 4, 2), ("x", "zl", "y", "zh", "c"))
    return jax.shard_map(
        body,
        mesh=fine,
        in_specs=(P(MODE, None, SPACE, None), P(None, SPACE, None), P()),
        out_specs=P(SPACE, MODE),
        check_vma=False,
    )
```

time: 99.7 us -> 108 us (1.083)
  blocking collectives: 32.9 us -> 0 us
  waiting for transfers between devices: 17 us -> 41.7 us
  starting transfers between devices: 23.2 us -> 47.8 us
  between operations: 6.48 us -> 0.21 us
  local copies, waits for them, and re-layouts: 4.89 us -> 1.25 us
  Pallas kernels: 10.6 us -> 13.3 us
    all_to_all x1 -> x0, blocking collectives: 32.9 us -> none  [body(): shares = lax.all_to_all(kept + other, ('y', 'zh'), 0, 0, tiled=True)]
    all_to_all x2 -> x4, waiting for transfers between devices: 13.1 us -> 38.2 us  [the longest x2 18.1 us: body(): shares.append(lax.all_to_all(kept + other, ('y', 'zh'), 0, 0, tiled=True))]
    all_to_all x2 -> x4, starting transfers between devices: 10.2 us -> 33.5 us  [the longest x2 24.1 us: body(): shares.append(lax.all_to_all(kept + other, ('y', 'zh'), 0, 0, tiled=True))]
    pallas_call x2 -> x6, Pallas kernels: 10.6 us -> 13.3 us  [the longest x4 10.2 us: project(): pl.pallas_call(lambda *refs: kernel(*refs, send=send, chunk=chunk), grid=...]
    ppermute x1 -> x2, starting transfers between devices: 1.91 us -> 4.13 us  [body(): other = lax.ppermute(sent, 'c', [(0, 1), (1, 0)])]
    unnamed x6 -> x7, local copies, waits for them, and re-layouts: 2.14 us -> 0.11 us
  transfers between devices with their start and end apart: 5 -> 8, of which waited for: 3 -> 5; matrix products, arithmetic and copies ran while one was open for 0% -> 1% of each run, Pallas kernels for 5% -> 7%
where the time goes in v2:
time: 108 us; the launch traced here: 106 us
  starting transfers between devices  47.8 us (44%)
  waiting for transfers between devices  41.7 us (39%)
  Pallas kernels  13.3 us (12%)
  other arithmetic  2.17 us (2%)
  local copies, waits for them, and re-layouts  1.25 us (1%)
    all_to_all x2, starting transfers between devices, body(): shares.append(lax.all_to_all(kept + other, ('y', 'zh'), 0, 0, tiled=True))  24.1 us
    all_to_all x2, waiting for transfers between devices, body(): shares.append(lax.all_to_all(kept + other, ('y', 'zh'), 0, 0, tiled=True))  18.1 us
    all_to_all x1, waiting for transfers between devices, body(): recv = lax.all_to_all(choose(plan, place, pieces), MODE, 0, 0, tiled=True)  10.9 us
    pallas_call x4, Pallas kernels, project(): pl.pallas_call(lambda *refs: kernel(*refs, send=send, chunk=chunk), grid=...  10.2 us
    all_to_all x1, waiting for transfers between devices, body(): lax.all_to_all(pack(plan, fields, low, high), MODE, 0, 0, tiled=True)  9.17 us
    ppermute x1, starting transfers between devices, body(): low = lax.ppermute(by_row[:, :, 3], SPACE, forward)  7.32 us
    all_to_all x1, starting transfers between devices, body(): lax.all_to_all(pack(plan, fields, low, high), MODE, 0, 0, tiled=True)  5.84 us
    ppermute x2, starting transfers between devices, body(): other = lax.ppermute(sent, 'c', [(0, 1), (1, 0)])  4.13 us
  transfers between devices with their start and end apart: 8, of which 5 were waited for; matrix products, arithmetic and copies ran while one was open for 1% of the time, Pallas kernels for 7%

profile of v2, /device:TPU:1, one launch (start us, length us, event | category | flops | bytes accessed | tf_op | source)
XLA Modules:
  0.0 106.4 jit_solution(1677130640219430547)
XLA Ops:
  0.0 1.0 copy.16
  1.0 0.0 copy-start.1
  1.0 7.3 %collective-permute-start = (bf16[8,2,8,256]{3,2,1,0:T(8,128)(2,1)S(1)}, bf16[8,2,8,256]{3,2,1,0:T(8,128)(2,1)S(1)}, u32[]{:S(2)}, u32[]{:S(2)}) collective-permute-start(bf16[8,2,8,256]{3,2,1,0:T(8,128)(2,1)S(1)} %get-tuple-element.6), channel_id=1, source_target_pairs={{0,1},{1,2},{2,3},{3,4},{4,5},{5,6},{6,7},{7,8},{8,9},{9,10},{10,1... | collective-permute-start | bytes 196616 | tf_op jit(solution)/shard_map/ppermute | solution.py:163
  8.4 0.0 copy-start.2
  8.4 2.9 %collective-permute-start.1 = (bf16[8,2,8,256]{3,2,1,0:T(8,128)(2,1)S(1)}, bf16[8,2,8,256]{3,2,1,0:T(8,128)(2,1)S(1)}, u32[]{:S(2)}, u32[]{:S(2)}) collective-permute-start(bf16[8,2,8,256]{3,2,1,0:T(8,128)(2,1)S(1)} %get-tuple-element.5), channel_id=1, source_target_pairs={{1,0},{2,1},{3,2},{4,3},{5,4},{6,5},{7,6},{8,7},{9,8},{10,9},{11,1... | collective-permute-start | bytes 196616 | tf_op jit(solution)/shard_map/ppermute | solution.py:164
  11.2 0.0 copy-done.1
  11.2 0.1 copy.14
  11.3 0.0 copy-done.2
  11.3 0.1 copy.11.plan_ref
  11.4 0.0 collective-permute-done.low_ref
  11.4 3.4 %collective-permute-done.1.high_ref = bf16[8,2,8,256]{3,2,1,0:T(8,128)(2,1)S(1)} collective-permute-done((bf16[8,2,8,256]{3,2,1,0:T(8,128)(2,1)S(1)}, bf16[8,2,8,256]{3,2,1,0:T(8,128)(2,1)S(1)}, u32[]{:S(2)}, u32[]{:S(2)}) %collective-permute-start.1) | collective-permute-done | bytes 65568 | tf_op jit(solution)/shard_map/ppermute | solution.py:164
  14.9 1.5 %pack.1 = bf16[8,20,8,256]{3,2,1,0:T(8,128)(2,1)} custom-call(s32[4,2]{1,0:T(4,128)S(1)} %copy.11.plan_ref, bf16[8,8,8,256]{3,2,1,0:T(8,128)(2,1)S(1)} %bitcast.13, bf16[8,2,8,256]{3,2,1,0:T(8,128)(2,1)S(1)} %collective-permute-done.low_ref, bf16[8,2,8,256]{3,2,1,0:T(8,128)(2,1)S(1)} %collective-permute-done.1.high_ref), custom_call_target="tpu_custom_call" | custom-call | tf_op jit(solution)/shard_map/pack/pallas_call | solution.py:43
  16.4 5.8 %all-to-all-start = ((bf16[8,20,8,256]{3,2,1,0:T(8,128)(2,1)}), bf16[8,20,8,256]{3,2,1,0:T(8,128)(2,1)S(1)}, u32[]{:S(2)}, u32[]{:S(2)}) async-start(bf16[8,20,8,256]{3,2,1,0:T(8,128)(2,1)} %pack.1), calls=%async_computation | async-start | bytes 1310720 | tf_op jit(solution)/shard_map/all_to_all | solution.py:165
  22.2 9.2 %all-to-all-done.pieces_ref = bf16[8,20,8,256]{3,2,1,0:T(8,128)(2,1)S(1)} async-done(((bf16[8,20,8,256]{3,2,1,0:T(8,128)(2,1)}), bf16[8,20,8,256]{3,2,1,0:T(8,128)(2,1)S(1)}, u32[]{:S(2)}, u32[]{:S(2)}) %all-to-all-start) | async-done | bytes 655392 | tf_op jit(solution)/shard_map/all_to_all | solution.py:165
  31.4 1.6 %choose.1 = bf16[8,20,8,256]{3,2,1,0:T(8,128)(2,1)} custom-call(s32[4,2]{1,0:T(4,128)S(1)} %copy.11.plan_ref, s32[1]{0:T(128)} %bitcast.1.place_ref, bf16[8,20,8,256]{3,2,1,0:T(8,128)(2,1)S(1)} %all-to-all-done.pieces_ref), custom_call_target="tpu_custom_call" | custom-call | tf_op jit(solution)/shard_map/choose/pallas_call | solution.py:69
  32.9 0.0 copy-start
  33.0 3.6 %all-to-all-start.1 = ((bf16[8,20,8,256]{3,2,1,0:T(8,128)(2,1)}), bf16[8,20,8,256]{3,2,1,0:T(8,128)(2,1)S(1)}, u32[]{:S(2)}, u32[]{:S(2)}) async-start(bf16[8,20,8,256]{3,2,1,0:T(8,128)(2,1)} %choose.1), calls=%async_computation.1 | async-start | bytes 1310720 | tf_op jit(solution)/shard_map/all_to_all | solution.py:167
  36.5 10.9 %all-to-all-done.1.refs_2_ = bf16[8,20,8,256]{3,2,1,0:T(8,128)(2,1)S(1)} async-done(((bf16[8,20,8,256]{3,2,1,0:T(8,128)(2,1)}), bf16[8,20,8,256]{3,2,1,0:T(8,128)(2,1)S(1)}, u32[]{:S(2)}, u32[]{:S(2)}) %all-to-all-start.1) | async-done | bytes 655392 | tf_op jit(solution)/shard_map/all_to_all | solution.py:167
  47.5 0.0 copy-done
  47.5 2.5 %project_1_send.1 = f32[32,16,128]{2,1,0:T(8,128)S(1)} custom-call(s32[1]{0:T(128)} %bitcast.refs_0_, f32[3,4,256]{2,1,0:T(4,128)S(1)} %copy-done, bf16[8,20,8,256]{3,2,1,0:T(8,128)(2,1)S(1)} %all-to-all-done.1.refs_2_, bf16[8,8,8,256]{3,2,1,0:T(8,128)(2,1)S(1)} %bitcast.14), custom_call_target="tpu_custom_call" | custom-call | tf_op jit(solution)/shard_map/project_1_send/pallas_call | solution.py:132
  50.0 1.9 %collective-permute-start.3 = (f32[32,16,128]{2,1,0:T(8,128)S(1)}, f32[32,16,128]{2,1,0:T(8,128)S(1)}, u32[]{:S(2)}, u32[]{:S(2)}) collective-permute-start(f32[32,16,128]{2,1,0:T(8,128)S(1)} %project_1_send.1), channel_id=1, source_target_pairs={{0,1},{1,0},{2,3},{3,2},{4,5},{5,4},{6,7},{7,6},{8,9},{9,8},{10,11... | collective-permute-start | bytes 786440 | tf_op jit(solution)/shard_map/ppermute | solution.py:173
  51.9 2.6 %project_1_keep.1 = f32[32,16,128]{2,1,0:T(8,128)S(1)} custom-call(s32[1]{0:T(128)} %bitcast.refs_0_, f32[3,4,256]{2,1,0:T(4,128)S(1)} %copy-done, bf16[8,20,8,256]{3,2,1,0:T(8,128)(2,1)S(1)} %all-to-all-done.1.refs_2_, bf16[8,8,8,256]{3,2,1,0:T(8,128)(2,1)S(1)} %bitcast.15), custom_call_target="tpu_custom_call" | custom-call | tf_op jit(solution)/shard_map/project_1_keep/pallas_call | solution.py:132
  54.5 0.0 collective-permute-done.3
  54.5 0.7 add.11
  55.2 17.2 %all-to-all-start.3 = ((f32[32,16,128]{2,1,0:T(8,128)}), f32[32,16,128]{2,1,0:T(8,128)S(1)}, u32[]{:S(2)}, u32[]{:S(2)}) async-start(f32[32,16,128]{2,1,0:T(8,128)} %add.11), calls=%async_computation.3 | async-start | bytes 524288 | tf_op jit(solution)/shard_map/all_to_all | solution.py:175
  72.5 2.5 %project_0_send.1 = f32[32,16,128]{2,1,0:T(8,128)S(1)} custom-call(s32[1]{0:T(128)} %bitcast.refs_0_, f32[3,4,256]{2,1,0:T(4,128)S(1)} %copy-done, bf16[8,20,8,256]{3,2,1,0:T(8,128)(2,1)S(1)} %all-to-all-done.1.refs_2_, bf16[8,8,8,256]{3,2,1,0:T(8,128)(2,1)S(1)} %bitcast.16), custom_call_target="tpu_custom_call" | custom-call | tf_op jit(solution)/shard_map/project_0_send/pallas_call | solution.py:132
  75.1 2.2 %collective-permute-start.2 = (f32[32,16,128]{2,1,0:T(8,128)S(1)}, f32[32,16,128]{2,1,0:T(8,128)S(1)}, u32[]{:S(2)}, u32[]{:S(2)}) collective-permute-start(f32[32,16,128]{2,1,0:T(8,128)S(1)} %project_0_send.1), channel_id=1, source_target_pairs={{0,1},{1,0},{2,3},{3,2},{4,5},{5,4},{6,7},{7,6},{8,9},{9,8},{10,11... | collective-permute-start | bytes 786440 | tf_op jit(solution)/shard_map/ppermute | solution.py:173
  77.3 2.6 %project_0_keep.1 = f32[32,16,128]{2,1,0:T(8,128)S(1)} custom-call(s32[1]{0:T(128)} %bitcast.refs_0_, f32[3,4,256]{2,1,0:T(4,128)S(1)} %copy-done, bf16[8,20,8,256]{3,2,1,0:T(8,128)(2,1)S(1)} %all-to-all-done.1.refs_2_, bf16[8,8,8,256]{3,2,1,0:T(8,128)(2,1)S(1)} %bitcast.17), custom_call_target="tpu_custom_call" | custom-call | tf_op jit(solution)/shard_map/project_0_keep/pallas_call | solution.py:132
  79.9 0.0 collective-permute-done.2
  79.9 0.7 add.10
  80.6 5.0 %all-to-all-done.3 = f32[32,16,128]{2,1,0:T(8,128)S(1)} async-done(((f32[32,16,128]{2,1,0:T(8,128)}), f32[32,16,128]{2,1,0:T(8,128)S(1)}, u32[]{:S(2)}, u32[]{:S(2)}) %all-to-all-start.3) | async-done | bytes 262176 | tf_op jit(solution)/shard_map/all_to_all | solution.py:175
  85.6 6.9 %all-to-all-start.2 = ((f32[32,16,128]{2,1,0:T(8,128)}), f32[32,16,128]{2,1,0:T(8,128)S(1)}, u32[]{:S(2)}, u32[]{:S(2)}) async-start(f32[32,16,128]{2,1,0:T(8,128)} %add.10), calls=%async_computation.2 | async-start | bytes 524288 | tf_op jit(solution)/shard_map/all_to_all | solution.py:175
  92.6 13.1 %all-to-all-done.2 = f32[32,16,128]{2,1,0:T(8,128)S(1)} async-done(((f32[32,16,128]{2,1,0:T(8,128)}), f32[32,16,128]{2,1,0:T(8,128)S(1)}, u32[]{:S(2)}, u32[]{:S(2)}) %all-to-all-start.2) | async-done | bytes 262176 | tf_op jit(solution)/shard_map/all_to_all | solution.py:175
  105.7 0.1 fusion
  105.8 0.6 pad_maximum_fusion
  (5 shorter events, 0.1 us)
Async XLA Ops:
  1.0 10.2 %copy-start.1 = (bf16[64,2,4,256]{3,2,1,0:T(4,128)(2,1)S(1)}, bf16[64,2,4,256]{3,2,1,0:T(4,128)(2,1)}, u32[]{:S(2)}) copy-start(bf16[64,2,4,256]{3,2,1,0:T(4,128)(2,1)} %param.3) | copy-start | bytes 786436
  1.0 10.4 %collective-permute-start = (bf16[8,2,8,256]{3,2,1,0:T(8,128)(2,1)S(1)}, bf16[8,2,8,256]{3,2,1,0:T(8,128)(2,1)S(1)}, u32[]{:S(2)}, u32[]{:S(2)}) collective-permute-start(bf16[8,2,8,256]{3,2,1,0:T(8,128)(2,1)S(1)} %get-tuple-element.6), channel_id=1, source_target_pairs={{0,1},{1,2},{2,3},{3,4},{4,5},{5,6},{6,7},{7,8},{8,9},{9,10},{10,1... | collective-permute-start | bytes 196616 | tf_op jit(solution)/shard_map/ppermute | solution.py:163
  8.4 2.9 %copy-start.2 = (s32[4,2]{0,1:T(2,128)S(1)}, s32[4,2]{0,1:T(2,128)}, u32[]{:S(2)}) copy-start(s32[4,2]{0,1:T(2,128)} %param.5) | copy-start | bytes 100
  8.4 6.5 %collective-permute-start.1 = (bf16[8,2,8,256]{3,2,1,0:T(8,128)(2,1)S(1)}, bf16[8,2,8,256]{3,2,1,0:T(8,128)(2,1)S(1)}, u32[]{:S(2)}, u32[]{:S(2)}) collective-permute-start(bf16[8,2,8,256]{3,2,1,0:T(8,128)(2,1)S(1)} %get-tuple-element.5), channel_id=1, source_target_pairs={{1,0},{2,1},{3,2},{4,3},{5,4},{6,5},{7,6},{8,7},{9,8},{10,9},{11,1... | collective-permute-start | bytes 196616 | tf_op jit(solution)/shard_map/ppermute | solution.py:164
  16.4 15.0 %all-to-all-start = ((bf16[8,20,8,256]{3,2,1,0:T(8,128)(2,1)}), bf16[8,20,8,256]{3,2,1,0:T(8,128)(2,1)S(1)}, u32[]{:S(2)}, u32[]{:S(2)}) async-start(bf16[8,20,8,256]{3,2,1,0:T(8,128)(2,1)} %pack.1), calls=%async_computation | async-start | bytes 1310720 | tf_op jit(solution)/shard_map/all_to_all | solution.py:165
  32.9 14.5 %copy-start = (f32[3,4,256]{2,1,0:T(4,128)S(1)}, f32[3,4,256]{2,1,0:T(4,128)}, u32[]{:S(2)}) copy-start(f32[3,4,256]{2,1,0:T(4,128)} %refs_1_.7) | copy-start | bytes 36868
  33.0 14.5 %all-to-all-start.1 = ((bf16[8,20,8,256]{3,2,1,0:T(8,128)(2,1)}), bf16[8,20,8,256]{3,2,1,0:T(8,128)(2,1)S(1)}, u32[]{:S(2)}, u32[]{:S(2)}) async-start(bf16[8,20,8,256]{3,2,1,0:T(8,128)(2,1)} %choose.1), calls=%async_computation.1 | async-start | bytes 1310720 | tf_op jit(solution)/shard_map/all_to_all | solution.py:167
  50.0 4.5 %collective-permute-start.3 = (f32[32,16,128]{2,1,0:T(8,128)S(1)}, f32[32,16,128]{2,1,0:T(8,128)S(1)}, u32[]{:S(2)}, u32[]{:S(2)}) collective-permute-start(f32[32,16,128]{2,1,0:T(8,128)S(1)} %project_1_send.1), channel_id=1, source_target_pairs={{0,1},{1,0},{2,3},{3,2},{4,5},{5,4},{6,7},{7,6},{8,9},{9,8},{10,11... | collective-permute-start | bytes 786440 | tf_op jit(solution)/shard_map/ppermute | solution.py:173
  55.2 30.4 %all-to-all-start.3 = ((f32[32,16,128]{2,1,0:T(8,128)}), f32[32,16,128]{2,1,0:T(8,128)S(1)}, u32[]{:S(2)}, u32[]{:S(2)}) async-start(f32[32,16,128]{2,1,0:T(8,128)} %add.11), calls=%async_computation.3 | async-start | bytes 524288 | tf_op jit(solution)/shard_map/all_to_all | solution.py:175
  75.1 4.8 %collective-permute-start.2 = (f32[32,16,128]{2,1,0:T(8,128)S(1)}, f32[32,16,128]{2,1,0:T(8,128)S(1)}, u32[]{:S(2)}, u32[]{:S(2)}) collective-permute-start(f32[32,16,128]{2,1,0:T(8,128)S(1)} %project_0_send.1), channel_id=1, source_target_pairs={{0,1},{1,0},{2,3},{3,2},{4,5},{5,4},{6,7},{7,6},{8,9},{9,8},{10,11... | collective-permute-start | bytes 786440 | tf_op jit(solution)/shard_map/ppermute | solution.py:173
  85.6 20.0 %all-to-all-start.2 = ((f32[32,16,128]{2,1,0:T(8,128)}), f32[32,16,128]{2,1,0:T(8,128)S(1)}, u32[]{:S(2)}, u32[]{:S(2)}) async-start(f32[32,16,128]{2,1,0:T(8,128)} %add.10), calls=%async_computation.2 | async-start | bytes 524288 | tf_op jit(solution)/shard_map/all_to_all | solution.py:175

commit v3 on v2

v3 whole, which is shorter than its diff:
```python
import jax
import jax.numpy as jnp
from jax import lax
from jax.experimental import pallas as pl
from jax.experimental.pallas import tpu as pltpu
from jax.sharding import Mesh, PartitionSpec as P

MODE = ("x", "zl")
SPACE = ("y", "zh", "c")
JB = 8
LIMIT = 16 * 2**20
SMEM = pl.BlockSpec(memory_space=pltpu.SMEM)
ANY = pl.BlockSpec(memory_space=pl.ANY)


def run_copies(pairs, sems):
    copies = [pltpu.make_async_copy(src, dst, sems.at[i]) for i, (src, dst) in enumerate(pairs)]
    for copy in copies:
        copy.start()
    for copy in copies:
        copy.wait()


def pack_kernel(plan_ref, fields_ref, out_ref, sems):
    half = fields_ref.shape[0] // 2
    pairs = []
    for b in range(2):
        here = pl.ds(b * half, half)
        mover = pl.ds(plan_ref[b, 1] * half, half)
        moved = pl.ds(plan_ref[2 + b, 1] * half, half)
        pairs += [
            (fields_ref.at[mover], out_ref.at[here, 0:8]),
            (fields_ref.at[moved], out_ref.at[here, 8:16]),
        ]
    run_copies(pairs, sems)


def pack(plan, fields):
    groups, _, m, ny = fields.shape
    return pl.pallas_call(
        pack_kernel,
        in_specs=[SMEM, ANY],
        out_specs=ANY,
        out_shape=jax.ShapeDtypeStruct((groups, 16, m, ny), fields.dtype),
        scratch_shapes=[pltpu.SemaphoreType.DMA((4,))],
        compiler_params=pltpu.CompilerParams(vmem_limit_bytes=LIMIT),
        name="pack",
    )(plan, fields)


def choose_kernel(plan_ref, place_ref, pieces_ref, out_ref, sems):
    groups = pieces_ref.shape[0]
    block = place_ref[0] // (groups // 2)
    mover = plan_ref[block, 0]
    moved = plan_ref[2 + block, 0]
    pairs = []
    for g in range(groups):
        pairs += [
            (pieces_ref.at[mover, 0:8], out_ref.at[g, 0:8]),
            (pieces_ref.at[moved, 8:16], out_ref.at[g, 8:16]),
        ]
    run_copies(pairs, sems)


def choose(plan, place, pieces):
    return pl.pallas_call(
        choose_kernel,
        in_specs=[SMEM, SMEM, ANY],
        out_specs=ANY,
        out_shape=jax.ShapeDtypeStruct(pieces.shape, pieces.dtype),
        scratch_shapes=[pltpu.SemaphoreType.DMA((16,))],
        compiler_params=pltpu.CompilerParams(vmem_limit_bytes=LIMIT),
        name="choose",
    )(plan, place, pieces)


def kernel(*refs, rows, edges):
    metric_any, recv_any, test_any, *refs = refs
    if edges:
        low_any, high_any, acc_ref, out_ref, low_ref, high_ref, *refs = refs
    else:
        out_ref, *refs = refs
    metric_ref, recv_ref, test_ref, s_ref, wm_ref, phi_ref, f_ref, sems = refs
    groups, _, m, ny = recv_ref.shape
    n = groups * m
    f32 = jnp.float32
    count = len(rows)

    def flat(block):
        return block.astype(f32).reshape(n, ny)

    def row(c, r):
        if r < 0:
            return flat(low_ref[:, c])
        if r > 3:
            return flat(high_ref[:, c])
        return flat(recv_ref[:, 8 + 4 * c + r])

    @pl.when(pl.program_id(0) == 0)
    def _():
        pairs = [(metric_any, metric_ref), (recv_any, recv_ref), (test_any, test_ref)]
        if edges:
            pairs += [(low_any, low_ref), (high_any, high_ref)]
        run_copies(pairs, sems)
        lane = lax.broadcasted_iota(jnp.int32, (n, ny), 1)
        for c in range(2):
            for i, r in enumerate(rows):
                at = count * c + i
                mid = row(c, r)
                along_x = (row(c, r + 1) - row(c, r - 1)) * metric_ref[0, pl.ds(r, 1), :]
                after = jnp.where(lane == ny - 1, 0.0, pltpu.roll(mid, ny - 1, 1))
                before = jnp.where(lane == 0, 0.0, pltpu.roll(mid, 1, 1))
                along_y = (after - before) * metric_ref[1, pl.ds(r, 1), :]
                s_ref[0, at] = along_x.astype(jnp.bfloat16).astype(f32)
                s_ref[1, at] = along_y.astype(jnp.bfloat16).astype(f32)
                wm_ref[at] = flat(recv_ref[:, 4 * c + r]) * metric_ref[2, pl.ds(r, 1), :]
                phi_ref[:, pl.ds(at * ny, ny)] = test_ref[:, 4 * c + r].reshape(n, ny)

    base = pl.program_id(0) * JB
    for c in range(2):
        for i in range(count):
            at = count * c + i
            s0 = s_ref[0, at]
            s1 = s_ref[1, at]
            for b in range(JB):
                j = pl.ds(base + b, 1)
                field = wm_ref[i, j, :] * s0 + wm_ref[count + i, j, :] * s1
                f_ref[pl.ds(b * n, n), pl.ds(at * ny, ny)] = field.astype(jnp.bfloat16)
    res = lax.dot_general(f_ref[...], phi_ref[...], (((1,), (1,)), ((), ())), preferred_element_type=f32)
    res = res.reshape(JB, n, n)
    res = jnp.concatenate([res[:, : n // 2], res[:, n // 2 :]], axis=2)
    if edges:
        res = res + acc_ref[...]
    out_ref[...] = res.astype(out_ref.dtype)


def project(metric, recv, test, rows, edges=None):
    groups, _, m, ny = recv.shape
    n = groups * m
    width = 2 * len(rows)
    block = pl.BlockSpec((JB, n // 2, 2 * n), lambda i: (i, 0, 0))
    scratch = [
        pltpu.VMEM(metric.shape, metric.dtype),
        pltpu.VMEM(recv.shape, recv.dtype),
        pltpu.VMEM(test.shape, test.dtype),
        pltpu.VMEM((2, width, n, ny), jnp.float32),
        pltpu.VMEM((width, n, ny), jnp.float32),
        pltpu.VMEM((n, width * ny), jnp.bfloat16),
        pltpu.VMEM((JB * n, width * ny), jnp.bfloat16),
        pltpu.SemaphoreType.DMA((5,)),
    ]
    args = [metric, recv, test]
    specs = [ANY, ANY, ANY]
    if edges:
        args += edges
        specs += [ANY, ANY, block]
        scratch = [pltpu.VMEM(edges[0].shape, edges[0].dtype), pltpu.VMEM(edges[1].shape, edges[1].dtype)] + scratch
    return pl.pallas_call(
        lambda *refs: kernel(*refs, rows=rows, edges=bool(edges)),
        grid=(n // JB,),
        in_specs=specs,
        out_specs=block,
        out_shape=jax.ShapeDtypeStruct((n, n // 2, 2 * n), jnp.bfloat16 if edges else jnp.float32),
        scratch_shapes=scratch,
        compiler_params=pltpu.CompilerParams(dimension_semantics=("arbitrary",), vmem_limit_bytes=LIMIT),
        name="project_edges" if edges else "project_middle",
    )(*args)


def body(mode_fields, metric, plan):
    n = mode_fields.shape[0]
    ny = mode_fields.shape[3]
    groups = lax.axis_size(MODE)
    m = n // groups
    fields = mode_fields.reshape(groups, m, 2, 4, ny).transpose(0, 2, 3, 1, 4).reshape(groups, 8, m, ny)
    pieces = lax.all_to_all(pack(plan, fields), MODE, 0, 0, tiled=True)
    place = lax.axis_index(MODE).astype(jnp.int32).reshape(1)
    recv = lax.all_to_all(choose(plan, place, pieces), MODE, 0, 0, tiled=True)
    count = lax.axis_size(SPACE)
    forward = [(i, i + 1) for i in range(count - 1)]
    backward = [(i + 1, i) for i in range(count - 1)]
    carried = recv[:, 8:].reshape(groups, 2, 4, m, ny)
    low = lax.ppermute(carried[:, :, 3], SPACE, forward)
    high = lax.ppermute(carried[:, :, 0], SPACE, backward)
    middle = project(metric, recv, fields, (1, 2))
    shares = project(metric, recv, fields, (0, 3), [low, high, middle])
    shares = lax.all_to_all(shares, SPACE, 0, 0, tiled=True)
    norm_factor = float(4 * count * ny) ** (-0.5)
    total = jnp.sum(shares.astype(jnp.float32), axis=0) * norm_factor
    return jnp.concatenate([total[:, :n], total[:, n:]], axis=0)


def solution(mesh):
    fine = Mesh(mesh.devices.reshape(4, 2, 8, 4, 2), ("x", "zl", "y", "zh", "c"))
    return jax.shard_map(
        body,
        mesh=fine,
        in_specs=(P(MODE, None, SPACE, None), P(None, SPACE, None), P()),
        out_specs=P(SPACE, MODE),
        check_vma=False,
    )
```

time: 108 us -> 85 us (0.79); the launches traced: 106 us -> 84.7 us
  blocking collectives: 0 us -> 43.1 us
  waiting for transfers between devices: 41.7 us -> 7.54 us
  starting transfers between devices: 47.8 us -> 19.3 us
  other arithmetic: 2.17 us -> 0.73 us
  Pallas kernels: 13.3 us -> 12 us
    all_to_all x0 -> x2, blocking collectives: none -> 43.1 us  [the longest x1 33 us: body(): shares = lax.all_to_all(shares, SPACE, 0, 0, tiled=True)]
    all_to_all x4 -> x1, waiting for transfers between devices: 38.2 us -> 7.54 us  [body(): pieces = lax.all_to_all(pack(plan, fields), MODE, 0, 0, tiled=True)]
    all_to_all x4 -> x1, starting transfers between devices: 33.5 us -> 6.66 us  [body(): pieces = lax.all_to_all(pack(plan, fields), MODE, 0, 0, tiled=True)]
    ppermute x4 -> x2, waiting for transfers between devices: 3.45 us -> 0.01 us  [the longest x1 0.01 us: body(): high = lax.ppermute(carried[:, :, 0], SPACE, backward)]
    ppermute x4 -> x2, starting transfers between devices: 14.3 us -> 12.7 us  [the longest x1 7.79 us: body(): high = lax.ppermute(carried[:, :, 0], SPACE, backward)]
    add x2 -> x0, other arithmetic: 1.47 us -> none  [body(): shares.append(lax.all_to_all(kept + other, ('y', 'zh'), 0, 0, tiled=True))]
    pallas_call x5 -> x3, Pallas kernels: 11.7 us -> 10.6 us  [the longest x2 9.18 us: project(): pl.pallas_call(lambda *refs: kernel(*refs, rows=rows, edges=bool(edges)),...]
  transfers between devices with their start and end apart: 8 -> 3, of which waited for: 5 -> 1; matrix products, arithmetic and copies ran while one was open for 1% -> 0% of each run, Pallas kernels for 7% -> 5%
where the time goes in v3:
time: 85 us; the launch traced here: 84.7 us
  blocking collectives  43.1 us (51%)
  starting transfers between devices  19.3 us (23%)
  Pallas kernels  12 us (14%)
  waiting for transfers between devices  7.54 us (9%)
  local copies, waits for them, and re-layouts  1.88 us (2%)
    all_to_all x1, blocking collectives, body(): shares = lax.all_to_all(shares, SPACE, 0, 0, tiled=True)  33 us
    all_to_all x1, blocking collectives, body(): recv = lax.all_to_all(choose(plan, place, pieces), MODE, 0, 0, tiled=True)  10.1 us
    pallas_call x2, Pallas kernels, project(): pl.pallas_call(lambda *refs: kernel(*refs, rows=rows, edges=bool(edges)),...  9.18 us
    ppermute x1, starting transfers between devices, body(): high = lax.ppermute(carried[:, :, 0], SPACE, backward)  7.79 us
    all_to_all x1, waiting for transfers between devices, body(): pieces = lax.all_to_all(pack(plan, fields), MODE, 0, 0, tiled=True)  7.54 us
    all_to_all x1, starting transfers between devices, body(): pieces = lax.all_to_all(pack(plan, fields), MODE, 0, 0, tiled=True)  6.66 us
    ppermute x1, starting transfers between devices, body(): low = lax.ppermute(carried[:, :, 3], SPACE, forward)  4.88 us
  transfers between devices with their start and end apart: 3, of which 1 were waited for; matrix products, arithmetic and copies ran while one was open for 0% of the time, Pallas kernels for 5%

profile of v3, /device:TPU:1, one launch (start us, length us, event | category | flops | bytes accessed | tf_op | source)
XLA Modules:
  0.0 84.7 jit_solution(12913551488102991864)
XLA Ops:
  0.0 0.8 copy.9.plan_ref
  0.8 1.0 %copy.7 = bf16[8,8,2,4,256]{4,1,3,2,0:T(8,128)(2,1)S(1)} copy(bf16[8,8,2,4,256]{4,3,2,1,0:T(4,128)(2,1)} %bitcast.18) | data formatting | bytes 524288 | tf_op jit(solution)/shard_map/reshape | solution.py:175
  1.8 1.4 %pack.1 = bf16[8,16,8,256]{3,2,1,0:T(8,128)(2,1)} custom-call(s32[4,2]{1,0:T(4,128)S(1)} %copy.9.plan_ref, bf16[8,8,8,256]{3,2,1,0:T(8,128)(2,1)S(1)} %bitcast.14), custom_call_target="tpu_custom_call" | custom-call | tf_op jit(solution)/shard_map/pack/pallas_call | solution.py:40
  3.2 6.7 %all-to-all-start = ((bf16[8,16,8,256]{3,2,1,0:T(8,128)(2,1)}), bf16[8,16,8,256]{3,2,1,0:T(8,128)(2,1)S(1)}, u32[]{:S(2)}, u32[]{:S(2)}) async-start(bf16[8,16,8,256]{3,2,1,0:T(8,128)(2,1)} %pack.1), calls=%async_computation | async-start | bytes 1048576 | tf_op jit(solution)/shard_map/all_to_all | solution.py:176
  9.8 7.5 %all-to-all-done.pieces_ref = bf16[8,16,8,256]{3,2,1,0:T(8,128)(2,1)S(1)} async-done(((bf16[8,16,8,256]{3,2,1,0:T(8,128)(2,1)}), bf16[8,16,8,256]{3,2,1,0:T(8,128)(2,1)S(1)}, u32[]{:S(2)}, u32[]{:S(2)}) %all-to-all-start) | async-done | bytes 524320 | tf_op jit(solution)/shard_map/all_to_all | solution.py:176
  17.4 1.4 %choose.1 = bf16[8,16,8,256]{3,2,1,0:T(8,128)(2,1)S(1)} custom-call(s32[4,2]{1,0:T(4,128)S(1)} %copy.9.plan_ref, s32[1]{0:T(128)} %bitcast.place_ref, bf16[8,16,8,256]{3,2,1,0:T(8,128)(2,1)S(1)} %all-to-all-done.pieces_ref), custom_call_target="tpu_custom_call" | custom-call | tf_op jit(solution)/shard_map/choose/pallas_call | solution.py:66
  18.8 10.1 %all_to_all.15.refs_1_ = bf16[8,16,8,256]{3,2,1,0:T(8,128)(2,1)S(1)} all-to-all(bf16[8,16,8,256]{3,2,1,0:T(8,128)(2,1)S(1)} %choose.1), channel_id=1, replica_groups=mesh['x'=4,'zl'=2,'y'=8,'zh'=4,'c'=2] {'x','zl'}, dimensions={0} | all-to-all | bytes 1048576 | tf_op jit(solution)/shard_map/all_to_all | solution.py:178
  28.9 0.0 copy-start
  28.9 7.8 %collective-permute-start.1 = (bf16[8,2,8,256]{3,2,1,0:T(8,128)(2,1)S(1)}, bf16[8,2,8,256]{3,2,1,0:T(8,128)(2,1)S(1)}, u32[]{:S(2)}, u32[]{:S(2)}) collective-permute-start(bf16[8,2,8,256]{3,2,1,0:T(8,128)(2,1)S(1)} %get-tuple-element.5), channel_id=1, source_target_pairs={{1,0},{2,1},{3,2},{4,3},{5,4},{6,5},{7,6},{8,7},{9,8},{10,9},{11,1... | collective-permute-start | bytes 196616 | tf_op jit(solution)/shard_map/ppermute | solution.py:184
  36.7 4.9 %collective-permute-start = (bf16[8,2,8,256]{3,2,1,0:T(8,128)(2,1)S(1)}, bf16[8,2,8,256]{3,2,1,0:T(8,128)(2,1)S(1)}, u32[]{:S(2)}, u32[]{:S(2)}) collective-permute-start(bf16[8,2,8,256]{3,2,1,0:T(8,128)(2,1)S(1)} %get-tuple-element.6), channel_id=1, source_target_pairs={{0,1},{1,2},{2,3},{3,4},{4,5},{5,6},{6,7},{7,8},{8,9},{9,10},{10,1... | collective-permute-start | bytes 196616 | tf_op jit(solution)/shard_map/ppermute | solution.py:183
  41.6 0.0 copy-done
  41.6 4.5 %project_middle.1.refs_5_ = f32[64,32,128]{2,1,0:T(8,128)S(1)} custom-call(f32[3,4,256]{2,1,0:T(4,128)S(1)} %copy-done, bf16[8,16,8,256]{3,2,1,0:T(8,128)(2,1)S(1)} %all_to_all.15.refs_1_, bf16[8,8,8,256]{3,2,1,0:T(8,128)(2,1)S(1)} %bitcast.15), custom_call_target="tpu_custom_call" | custom-call | tf_op jit(solution)/shard_map/project_middle/pallas_call | solution.py:158
  46.1 0.0 collective-permute-done.1.refs_4_
  46.1 0.0 collective-permute-done.refs_3_
  46.2 4.7 %project_edges.1 = bf16[64,32,128]{2,1,0:T(8,128)(2,1)S(1)} custom-call(f32[3,4,256]{2,1,0:T(4,128)S(1)} %copy-done, bf16[8,16,8,256]{3,2,1,0:T(8,128)(2,1)S(1)} %all_to_all.15.refs_1_, bf16[8,8,8,256]{3,2,1,0:T(8,128)(2,1)S(1)} %bitcast.16, bf16[8,2,8,256]{3,2,1,0:T(8,128)(2,1)S(1)} %collective-permute-done.refs_3_, ...), custom_call_target="tpu_custom_call" | custom-call | tf_op jit(solution)/shard_map/project_edges/pallas_call | solution.py:158
  50.9 33.0 %all_to_all.16 = bf16[64,32,128]{2,1,0:T(8,128)(2,1)S(1)} all-to-all(bf16[64,32,128]{2,1,0:T(8,128)(2,1)S(1)} %project_edges.1), channel_id=1, replica_groups=mesh['x'=4,'zl'=2,'y'=8,'zh'=4,'c'=2] {'y','zh','c'}, dimensions={0} | all-to-all | bytes 1048576 | tf_op jit(solution)/shard_map/all_to_all | solution.py:187
  83.9 0.1 convert_reduce_fusion
  84.0 0.1 fusion
  84.1 0.6 pad_maximum_fusion
  (3 shorter events, 0.0 us)
Async XLA Ops:
  3.2 14.2 %all-to-all-start = ((bf16[8,16,8,256]{3,2,1,0:T(8,128)(2,1)}), bf16[8,16,8,256]{3,2,1,0:T(8,128)(2,1)S(1)}, u32[]{:S(2)}, u32[]{:S(2)}) async-start(bf16[8,16,8,256]{3,2,1,0:T(8,128)(2,1)} %pack.1), calls=%async_computation | async-start | bytes 1048576 | tf_op jit(solution)/shard_map/all_to_all | solution.py:176
  28.9 12.7 %copy-start = (f32[3,4,256]{2,1,0:T(4,128)S(1)}, f32[3,4,256]{2,1,0:T(4,128)}, u32[]{:S(2)}) copy-start(f32[3,4,256]{2,1,0:T(4,128)} %refs_0_.3) | copy-start | bytes 36868
  28.9 17.2 %collective-permute-start.1 = (bf16[8,2,8,256]{3,2,1,0:T(8,128)(2,1)S(1)}, bf16[8,2,8,256]{3,2,1,0:T(8,128)(2,1)S(1)}, u32[]{:S(2)}, u32[]{:S(2)}) collective-permute-start(bf16[8,2,8,256]{3,2,1,0:T(8,128)(2,1)S(1)} %get-tuple-element.5), channel_id=1, source_target_pairs={{1,0},{2,1},{3,2},{4,3},{5,4},{6,5},{7,6},{8,7},{9,8},{10,9},{11,1... | collective-permute-start | bytes 196616 | tf_op jit(solution)/shard_map/ppermute | solution.py:184
  36.7 9.4 %collective-permute-start = (bf16[8,2,8,256]{3,2,1,0:T(8,128)(2,1)S(1)}, bf16[8,2,8,256]{3,2,1,0:T(8,128)(2,1)S(1)}, u32[]{:S(2)}, u32[]{:S(2)}) collective-permute-start(bf16[8,2,8,256]{3,2,1,0:T(8,128)(2,1)S(1)} %get-tuple-element.6), channel_id=1, source_target_pairs={{0,1},{1,2},{2,3},{3,4},{4,5},{5,6},{6,7},{7,8},{8,9},{9,10},{10,1... | collective-permute-start | bytes 196616 | tf_op jit(solution)/shard_map/ppermute | solution.py:183

commit v4 on v3

v4 whole, which is shorter than its diff:
```python
import jax
import jax.numpy as jnp
from jax import lax
from jax.experimental import pallas as pl
from jax.experimental.pallas import tpu as pltpu
from jax.sharding import Mesh, PartitionSpec as P

MODE = ("x", "zl")
SPACE = ("y", "zh", "c")
JB = 8
LIMIT = 16 * 2**20
SMEM = pl.BlockSpec(memory_space=pltpu.SMEM)
VMEM = pl.BlockSpec(memory_space=pltpu.VMEM)


def pack_kernel(plan_ref, place_ref, fields_ref, out_ref):
    del place_ref
    groups, _, m, ny = fields_ref.shape
    half = groups // 2
    for b in range(2):
        mover = plan_ref[1, b] * half
        moved = plan_ref[1, 2 + b] * half
        for g in range(half):
            out_ref[b * half + g, 0:8] = fields_ref[mover + g]
            out_ref[b * half + g, 8:16] = fields_ref[moved + g]


def pack(plan, place, fields):
    groups, _, m, ny = fields.shape
    return pl.pallas_call(
        pack_kernel,
        in_specs=[SMEM, SMEM, VMEM],
        out_specs=VMEM,
        out_shape=jax.ShapeDtypeStruct((groups, 16, m, ny), fields.dtype),
        compiler_params=pltpu.CompilerParams(vmem_limit_bytes=LIMIT),
        name="pack",
    )(plan, place, fields)


def choose_kernel(plan_ref, place_ref, pieces_ref, out_ref):
    groups = pieces_ref.shape[0]
    block = place_ref[0] // (groups // 2)
    mover = pieces_ref[plan_ref[0, block], 0:8]
    moved = pieces_ref[plan_ref[0, 2 + block], 8:16]
    for g in range(groups):
        out_ref[g, 0:8] = mover
        out_ref[g, 8:16] = moved


def choose(plan, place, pieces):
    return pl.pallas_call(
        choose_kernel,
        in_specs=[SMEM, SMEM, VMEM],
        out_specs=VMEM,
        out_shape=jax.ShapeDtypeStruct(pieces.shape, pieces.dtype),
        compiler_params=pltpu.CompilerParams(vmem_limit_bytes=LIMIT),
        name="choose",
    )(plan, place, pieces)


def kernel(*refs, rows, edges):
    metric_ref, recv_ref, test_ref, *refs = refs
    if edges:
        low_ref, high_ref, acc_ref, *refs = refs
    out_ref, s_ref, wm_ref, phi_ref, f_ref = refs
    groups, _, m, ny = recv_ref.shape
    n = groups * m
    f32 = jnp.float32
    count = len(rows)

    def flat(block):
        return block.astype(f32).reshape(n, ny)

    def row(c, r):
        if r < 0:
            return flat(low_ref[:, c])
        if r > 3:
            return flat(high_ref[:, c])
        return flat(recv_ref[:, 8 + 4 * c + r])

    @pl.when(pl.program_id(0) == 0)
    def _():
        lane = lax.broadcasted_iota(jnp.int32, (n, ny), 1)
        for c in range(2):
            for i, r in enumerate(rows):
                at = count * c + i
                mid = row(c, r)
                along_x = (row(c, r + 1) - row(c, r - 1)) * metric_ref[0, pl.ds(r, 1), :]
                after = jnp.where(lane == ny - 1, 0.0, pltpu.roll(mid, ny - 1, 1))
                before = jnp.where(lane == 0, 0.0, pltpu.roll(mid, 1, 1))
                along_y = (after - before) * metric_ref[1, pl.ds(r, 1), :]
                s_ref[0, at] = along_x.astype(jnp.bfloat16).astype(f32)
                s_ref[1, at] = along_y.astype(jnp.bfloat16).astype(f32)
                wm_ref[at] = flat(recv_ref[:, 4 * c + r]) * metric_ref[2, pl.ds(r, 1), :]
                phi_ref[:, pl.ds(at * ny, ny)] = test_ref[:, 4 * c + r].reshape(n, ny)

    base = pl.program_id(0) * JB
    for c in range(2):
        for i in range(count):
            at = count * c + i
            s0 = s_ref[0, at]
            s1 = s_ref[1, at]
            for b in range(JB):
                j = pl.ds(base + b, 1)
                field = wm_ref[i, j, :] * s0 + wm_ref[count + i, j, :] * s1
                f_ref[pl.ds(b * n, n), pl.ds(at * ny, ny)] = field.astype(jnp.bfloat16)
    res = lax.dot_general(f_ref[...], phi_ref[...], (((1,), (1,)), ((), ())), preferred_element_type=f32)
    res = res.reshape(JB, n, n)
    res = jnp.concatenate([res[:, : n // 2], res[:, n // 2 :]], axis=2)
    here = pl.ds(base, JB)
    if edges:
        res = res + acc_ref[here]
    out_ref[here] = res.astype(out_ref.dtype)


def project(metric, recv, test, rows, edges=None):
    groups, _, m, ny = recv.shape
    n = groups * m
    width = 2 * len(rows)
    args = [metric, recv, test] + (edges or [])
    return pl.pallas_call(
        lambda *refs: kernel(*refs, rows=rows, edges=bool(edges)),
        grid=(n // JB,),
        in_specs=[VMEM] * len(args),
        out_specs=VMEM,
        out_shape=jax.ShapeDtypeStruct((n, n // 2, 2 * n), jnp.bfloat16 if edges else jnp.float32),
        scratch_shapes=[
            pltpu.VMEM((2, width, n, ny), jnp.float32),
            pltpu.VMEM((width, n, ny), jnp.float32),
            pltpu.VMEM((n, width * ny), jnp.bfloat16),
            pltpu.VMEM((JB * n, width * ny), jnp.bfloat16),
        ],
        compiler_params=pltpu.CompilerParams(dimension_semantics=("arbitrary",), vmem_limit_bytes=LIMIT),
        name="project_edges" if edges else "project_middle",
    )(*args)


def body(mode_fields, metric, plan):
    n = mode_fields.shape[0]
    ny = mode_fields.shape[3]
    groups = lax.axis_size(MODE)
    m = n // groups
    fields = mode_fields.reshape(groups, m, 2, 4, ny).transpose(0, 2, 3, 1, 4).reshape(groups, 8, m, ny)
    place = lax.axis_index(MODE).astype(jnp.int32).reshape(1)
    pieces = lax.all_to_all(pack(plan.T, place, fields), MODE, 0, 0, tiled=True)
    recv = lax.all_to_all(choose(plan.T, place, pieces), MODE, 0, 0, tiled=True)
    count = lax.axis_size(SPACE)
    forward = [(i, i + 1) for i in range(count - 1)]
    backward = [(i + 1, i) for i in range(count - 1)]
    carried = recv[:, 8:].reshape(groups, 2, 4, m, ny)
    low = lax.ppermute(carried[:, :, 3], SPACE, forward)
    high = lax.ppermute(carried[:, :, 0], SPACE, backward)
    middle = project(metric, recv, fields, (1, 2))
    shares = project(metric, recv, fields, (0, 3), [low, high, middle])
    shares = lax.all_to_all(shares, SPACE, 0, 0, tiled=True)
    norm_factor = float(4 * count * ny) ** (-0.5)
    total = jnp.sum(shares.astype(jnp.float32), axis=0) * norm_factor
    return jnp.concatenate([total[:, :n], total[:, n:]], axis=0)


def solution(mesh):
    fine = Mesh(mesh.devices.reshape(4, 2, 8, 4, 2), ("x", "zl", "y", "zh", "c"))
    return jax.shard_map(
        body,
        mesh=fine,
        in_specs=(P(MODE, None, SPACE, None), P(None, SPACE, None), P()),
        out_specs=P(SPACE, MODE),
        check_vma=False,
    )
```

time: 85 us -> 82.8 us (0.974)
  blocking collectives: 43.1 us -> 56.9 us
  waiting for transfers between devices: 7.54 us -> 0.01 us
  starting transfers between devices: 19.3 us -> 12.8 us
  Pallas kernels: 12 us -> 10.1 us
    all_to_all x1 -> x2, blocking collectives: 10.1 us -> 23.9 us  [the longest x1 14 us: body(): pieces = lax.all_to_all(pack(plan.T, place, fields), MODE, 0, 0, tiled=True)]
    all_to_all x1 -> x0, waiting for transfers between devices: 7.54 us -> none  [body(): pieces = lax.all_to_all(pack(plan, fields), MODE, 0, 0, tiled=True)]
    all_to_all x1 -> x0, starting transfers between devices: 6.66 us -> none  [body(): pieces = lax.all_to_all(pack(plan, fields), MODE, 0, 0, tiled=True)]
    pallas_call x2, Pallas kernels: 2.83 us -> 1.18 us  [the longest x1 0.59 us: choose(): pl.pallas_call(choose_kernel, in_specs=[SMEM, SMEM, VMEM], out_specs=VMEM...]
  transfers between devices with their start and end apart: 3 -> 2, of which waited for: 1 -> 0; matrix products, arithmetic and copies ran while one was open for 0% -> 0% of each run, Pallas kernels for 5% -> 5%
where the time goes in v4:
time: 82.8 us; the launch traced here: 82.4 us
  blocking collectives  56.9 us (69%)
  starting transfers between devices  12.8 us (15%)
  Pallas kernels  10.1 us (12%)
  local copies, waits for them, and re-layouts  1.79 us (2%)
    all_to_all x1, blocking collectives, body(): shares = lax.all_to_all(shares, SPACE, 0, 0, tiled=True)  33 us
    all_to_all x1, blocking collectives, body(): pieces = lax.all_to_all(pack(plan.T, place, fields), MODE, 0, 0, tiled=True)  14 us
    all_to_all x1, blocking collectives, body(): recv = lax.all_to_all(choose(plan.T, place, pieces), MODE, 0, 0, tiled=True)  9.95 us
    pallas_call x2, Pallas kernels, project(): pl.pallas_call(lambda *refs: kernel(*refs, rows=rows, edges=bool(edges)),...  8.88 us
    ppermute x1, starting transfers between devices, body(): high = lax.ppermute(carried[:, :, 0], SPACE, backward)  7.12 us
    ppermute x1, starting transfers between devices, body(): low = lax.ppermute(carried[:, :, 3], SPACE, forward)  5.72 us
  transfers between devices with their start and end apart: 2, of which 0 were waited for; matrix products, arithmetic and copies ran while one was open for 0% of the time, Pallas kernels for 5%

profile of v4, /device:TPU:1, one launch (start us, length us, event | category | flops | bytes accessed | tf_op | source)
XLA Modules:
  0.0 82.4 jit_solution(1360076169217358306)
XLA Ops:
  0.0 1.0 %copy.5 = bf16[8,8,2,4,256]{4,1,3,2,0:T(8,128)(2,1)S(1)} copy(bf16[8,8,2,4,256]{4,3,2,1,0:T(4,128)(2,1)} %bitcast.21) | data formatting | bytes 524288 | tf_op jit(solution)/shard_map/reshape | solution.py:143
  1.0 0.0 copy-start.1
  1.0 0.7 copy-done.1
  1.7 0.6 pack.1
  2.3 14.0 %all_to_all.15.pieces_ref = bf16[8,16,8,256]{3,2,1,0:T(8,128)(2,1)S(1)} all-to-all(bf16[8,16,8,256]{3,2,1,0:T(8,128)(2,1)S(1)} %pack.1), channel_id=1, replica_groups=mesh['x'=4,'zl'=2,'y'=8,'zh'=4,'c'=2] {'x','zl'}, dimensions={0} | all-to-all | bytes 1048576 | tf_op jit(solution)/shard_map/all_to_all | solution.py:145
  16.3 0.6 choose.1
  16.9 10.0 %all_to_all.16.refs_1_ = bf16[8,16,8,256]{3,2,1,0:T(8,128)(2,1)S(1)} all-to-all(bf16[8,16,8,256]{3,2,1,0:T(8,128)(2,1)S(1)} %choose.1), channel_id=1, replica_groups=mesh['x'=4,'zl'=2,'y'=8,'zh'=4,'c'=2] {'x','zl'}, dimensions={0} | all-to-all | bytes 1048576 | tf_op jit(solution)/shard_map/all_to_all | solution.py:146
  26.8 0.0 copy-start
  26.9 7.1 %collective-permute-start.1 = (bf16[8,2,8,256]{3,2,1,0:T(8,128)(2,1)S(1)}, bf16[8,2,8,256]{3,2,1,0:T(8,128)(2,1)S(1)}, u32[]{:S(2)}, u32[]{:S(2)}) collective-permute-start(bf16[8,2,8,256]{3,2,1,0:T(8,128)(2,1)S(1)} %get-tuple-element.5), channel_id=1, source_target_pairs={{1,0},{2,1},{3,2},{4,3},{5,4},{6,5},{7,6},{8,7},{9,8},{10,9},{11,1... | collective-permute-start | bytes 196616 | tf_op jit(solution)/shard_map/ppermute | solution.py:152
  34.0 5.7 %collective-permute-start = (bf16[8,2,8,256]{3,2,1,0:T(8,128)(2,1)S(1)}, bf16[8,2,8,256]{3,2,1,0:T(8,128)(2,1)S(1)}, u32[]{:S(2)}, u32[]{:S(2)}) collective-permute-start(bf16[8,2,8,256]{3,2,1,0:T(8,128)(2,1)S(1)} %get-tuple-element.6), channel_id=1, source_target_pairs={{0,1},{1,2},{2,3},{3,4},{4,5},{5,6},{6,7},{7,8},{8,9},{9,10},{10,1... | collective-permute-start | bytes 196616 | tf_op jit(solution)/shard_map/ppermute | solution.py:151
  39.7 0.0 copy-done
  39.7 4.4 %project_middle.1.refs_5_ = f32[64,32,128]{2,1,0:T(8,128)S(1)} custom-call(f32[3,4,256]{2,1,0:T(4,128)S(1)} %copy-done, bf16[8,16,8,256]{3,2,1,0:T(8,128)(2,1)S(1)} %all_to_all.16.refs_1_, bf16[8,8,8,256]{3,2,1,0:T(8,128)(2,1)S(1)} %bitcast.16), custom_call_target="tpu_custom_call" | custom-call | tf_op jit(solution)/shard_map/project_middle/pallas_call | solution.py:121
  44.2 0.0 collective-permute-done.1.refs_4_
  44.2 0.0 collective-permute-done.refs_3_
  44.2 4.4 %project_edges.1 = bf16[64,32,128]{2,1,0:T(8,128)(2,1)S(1)} custom-call(f32[3,4,256]{2,1,0:T(4,128)S(1)} %copy-done, bf16[8,16,8,256]{3,2,1,0:T(8,128)(2,1)S(1)} %all_to_all.16.refs_1_, bf16[8,8,8,256]{3,2,1,0:T(8,128)(2,1)S(1)} %bitcast.17, bf16[8,2,8,256]{3,2,1,0:T(8,128)(2,1)S(1)} %collective-permute-done.refs_3_, ...), custom_call_target="tpu_custom_call" | custom-call | tf_op jit(solution)/shard_map/project_edges/pallas_call | solution.py:121
  48.7 33.0 %all_to_all.17 = bf16[64,32,128]{2,1,0:T(8,128)(2,1)S(1)} all-to-all(bf16[64,32,128]{2,1,0:T(8,128)(2,1)S(1)} %project_edges.1), channel_id=1, replica_groups=mesh['x'=4,'zl'=2,'y'=8,'zh'=4,'c'=2] {'y','zh','c'}, dimensions={0} | all-to-all | bytes 1048576 | tf_op jit(solution)/shard_map/all_to_all | solution.py:155
  81.6 0.1 convert_reduce_fusion
  81.7 0.1 fusion
  81.8 0.6 pad_maximum_fusion
  (3 shorter events, 0.0 us)
Async XLA Ops:
  1.0 0.7 copy-start.1
  26.8 12.9 %copy-start = (f32[3,4,256]{2,1,0:T(4,128)S(1)}, f32[3,4,256]{2,1,0:T(4,128)}, u32[]{:S(2)}) copy-start(f32[3,4,256]{2,1,0:T(4,128)} %refs_0_.3) | copy-start | bytes 36868
  26.9 17.3 %collective-permute-start.1 = (bf16[8,2,8,256]{3,2,1,0:T(8,128)(2,1)S(1)}, bf16[8,2,8,256]{3,2,1,0:T(8,128)(2,1)S(1)}, u32[]{:S(2)}, u32[]{:S(2)}) collective-permute-start(bf16[8,2,8,256]{3,2,1,0:T(8,128)(2,1)S(1)} %get-tuple-element.5), channel_id=1, source_target_pairs={{1,0},{2,1},{3,2},{4,3},{5,4},{6,5},{7,6},{8,7},{9,8},{10,9},{11,1... | collective-permute-start | bytes 196616 | tf_op jit(solution)/shard_map/ppermute | solution.py:152
  34.0 10.2 %collective-permute-start = (bf16[8,2,8,256]{3,2,1,0:T(8,128)(2,1)S(1)}, bf16[8,2,8,256]{3,2,1,0:T(8,128)(2,1)S(1)}, u32[]{:S(2)}, u32[]{:S(2)}) collective-permute-start(bf16[8,2,8,256]{3,2,1,0:T(8,128)(2,1)S(1)} %get-tuple-element.6), channel_id=1, source_target_pairs={{0,1},{1,2},{2,3},{3,4},{4,5},{5,6},{6,7},{7,8},{8,9},{9,10},{10,1... | collective-permute-start | bytes 196616 | tf_op jit(solution)/shard_map/ppermute | solution.py:151

commit v5 on v4

v5 whole, which is shorter than its diff:
```python
import jax
import jax.numpy as jnp
from jax import lax
from jax.experimental import pallas as pl
from jax.experimental.pallas import tpu as pltpu
from jax.sharding import Mesh, PartitionSpec as P

MODE = ("x", "zl")
SPACE = ("y", "zh", "c")
JB = 8
LIMIT = 16 * 2**20
SMEM = pl.BlockSpec(memory_space=pltpu.SMEM)
VMEM = pl.BlockSpec(memory_space=pltpu.VMEM)


def pack_kernel(plan_ref, place_ref, fields_ref, out_ref):
    del place_ref
    groups, _, m, ny = fields_ref.shape
    half = groups // 2
    for b in range(2):
        mover = plan_ref[1, b] * half
        moved = plan_ref[1, 2 + b] * half
        for g in range(half):
            out_ref[b * half + g, 0:8] = fields_ref[mover + g]
            out_ref[b * half + g, 8:16] = fields_ref[moved + g]


def pack(plan, place, fields):
    groups, _, m, ny = fields.shape
    return pl.pallas_call(
        pack_kernel,
        in_specs=[SMEM, SMEM, VMEM],
        out_specs=VMEM,
        out_shape=jax.ShapeDtypeStruct((groups, 16, m, ny), fields.dtype),
        compiler_params=pltpu.CompilerParams(vmem_limit_bytes=LIMIT),
        name="pack",
    )(plan, place, fields)


def choose_kernel(plan_ref, place_ref, pieces_ref, out_ref):
    groups = pieces_ref.shape[0]
    block = place_ref[0] // groups
    mover = pieces_ref[plan_ref[0, block], 0:8]
    moved = pieces_ref[plan_ref[0, 2 + block], 8:16]
    for g in range(groups):
        out_ref[g, 0:8] = mover
        out_ref[g, 8:16] = moved


def choose(plan, place, pieces):
    return pl.pallas_call(
        choose_kernel,
        in_specs=[SMEM, SMEM, VMEM],
        out_specs=VMEM,
        out_shape=jax.ShapeDtypeStruct(pieces.shape, pieces.dtype),
        compiler_params=pltpu.CompilerParams(vmem_limit_bytes=LIMIT),
        name="choose",
    )(plan, place, pieces)


def edge_kernel(place_ref, recv_ref, inner_ref, outer_ref):
    core = place_ref[0] % 2
    for c in range(2):
        inner_ref[:, c] = recv_ref[:, 8 + 4 * c + 3 * (1 - core)]
        outer_ref[:, c] = recv_ref[:, 8 + 4 * c + 3 * core]


def edge_rows(place, recv):
    groups, _, m, ny = recv.shape
    shape = jax.ShapeDtypeStruct((groups, 2, m, ny), recv.dtype)
    return pl.pallas_call(
        edge_kernel,
        in_specs=[SMEM, VMEM],
        out_specs=[VMEM, VMEM],
        out_shape=[shape, shape],
        compiler_params=pltpu.CompilerParams(vmem_limit_bytes=LIMIT),
        name="edge_rows",
    )(place, recv)


def kernel(*refs, rows, edges):
    metric_ref, recv_ref, test_ref, *refs = refs
    if edges:
        place_ref, inner_ref, outer_ref, acc_ref, *refs = refs
        first = place_ref[0] % 2 == 0
    out_ref, s_ref, wm_ref, phi_ref, even_ref, odd_ref = refs
    groups, _, m, ny = recv_ref.shape
    n = groups * m
    f32 = jnp.float32
    count = len(rows)

    def flat(block):
        return block.astype(f32).reshape(n, ny)

    def row(c, r):
        if r < 0:
            return jnp.where(first, flat(outer_ref[:, c]), flat(inner_ref[:, c]))
        if r > 3:
            return jnp.where(first, flat(inner_ref[:, c]), flat(outer_ref[:, c]))
        return flat(recv_ref[:, 8 + 4 * c + r])

    lane = lax.broadcasted_iota(jnp.int32, (n, ny), 1)
    for c in range(2):
        for i, r in enumerate(rows):
            at = count * c + i
            mid = row(c, r)
            along_x = (row(c, r + 1) - row(c, r - 1)) * metric_ref[0, pl.ds(r, 1), :]
            after = jnp.where(lane == ny - 1, 0.0, pltpu.roll(mid, ny - 1, 1))
            before = jnp.where(lane == 0, 0.0, pltpu.roll(mid, 1, 1))
            along_y = (after - before) * metric_ref[1, pl.ds(r, 1), :]
            s_ref[0, at] = along_x.astype(jnp.bfloat16).astype(f32)
            s_ref[1, at] = along_y.astype(jnp.bfloat16).astype(f32)
            wm_ref[at] = flat(recv_ref[:, 4 * c + r]) * metric_ref[2, pl.ds(r, 1), :]
            phi_ref[:, pl.ds(at * ny, ny)] = test_ref[:, 4 * c + r].reshape(n, ny)

    def build(block, f_ref):
        for at in range(2 * count):
            i = at % count
            s0 = s_ref[0, at]
            s1 = s_ref[1, at]
            for b in range(JB):
                j = pl.ds(block * JB + b, 1)
                field = wm_ref[i, j, :] * s0 + wm_ref[count + i, j, :] * s1
                f_ref[pl.ds(b * n, n), pl.ds(at * ny, ny)] = field.astype(jnp.bfloat16)

    def multiply(block, f_ref):
        res = lax.dot_general(f_ref[...], phi_ref[...], (((1,), (1,)), ((), ())), preferred_element_type=f32)
        res = res.reshape(JB, n, n)
        res = jnp.concatenate([res[:, : n // 2], res[:, n // 2 :]], axis=2)
        here = pl.ds(block * JB, JB)
        if edges:
            res = res + acc_ref[here]
        out_ref[here] = res.astype(out_ref.dtype)

    blocks = n // JB
    buffers = (even_ref, odd_ref)
    build(0, even_ref)
    for block in range(blocks):
        if block + 1 < blocks:
            build(block + 1, buffers[(block + 1) % 2])
        multiply(block, buffers[block % 2])


def project(metric, recv, test, rows, edges=None):
    groups, _, m, ny = recv.shape
    n = groups * m
    width = 2 * len(rows)
    args = [metric, recv, test] + (edges or [])
    return pl.pallas_call(
        lambda *refs: kernel(*refs, rows=rows, edges=bool(edges)),
        in_specs=[VMEM] * 3 + ([SMEM] + [VMEM] * 3 if edges else []),
        out_specs=VMEM,
        out_shape=jax.ShapeDtypeStruct((n, n // 2, 2 * n), jnp.bfloat16 if edges else jnp.float32),
        scratch_shapes=[
            pltpu.VMEM((2, width, n, ny), jnp.float32),
            pltpu.VMEM((width, n, ny), jnp.float32),
            pltpu.VMEM((n, width * ny), jnp.bfloat16),
            pltpu.VMEM((JB * n, width * ny), jnp.bfloat16),
            pltpu.VMEM((JB * n, width * ny), jnp.bfloat16),
        ],
        compiler_params=pltpu.CompilerParams(vmem_limit_bytes=LIMIT),
        name="project_edges" if edges else "project_middle",
    )(*args)


def body(mode_fields, metric, plan):
    n = mode_fields.shape[0]
    ny = mode_fields.shape[3]
    groups = lax.axis_size(MODE)
    m = n // groups
    fields = mode_fields.reshape(groups, m, 2, 4, ny).transpose(0, 2, 3, 1, 4).reshape(groups, 8, m, ny)
    place = lax.axis_index(MODE + ("c",)).astype(jnp.int32).reshape(1)
    pieces = lax.all_to_all(pack(plan.T, place, fields), MODE, 0, 0, tiled=True)
    recv = lax.all_to_all(choose(plan.T, place, pieces), MODE, 0, 0, tiled=True)
    count = lax.axis_size(SPACE)
    inner, outer = edge_rows(place, recv)
    between = [(i, i + 1 if i % 2 else i - 1) for i in range(1, count - 1)]
    outer = lax.ppermute(outer, SPACE, between)
    inner = lax.ppermute(inner, "c", [(0, 1), (1, 0)])
    middle = project(metric, recv, fields, (1, 2))
    shares = project(metric, recv, fields, (0, 3), [place, inner, outer, middle])
    shares = lax.all_to_all(shares, SPACE, 0, 0, tiled=True)
    norm_factor = float(4 * count * ny) ** (-0.5)
    total = jnp.sum(shares.astype(jnp.float32), axis=0) * norm_factor
    return jnp.concatenate([total[:, :n], total[:, n:]], axis=0)


def solution(mesh):
    fine = Mesh(mesh.devices.reshape(4, 2, 8, 4, 2), ("x", "zl", "y", "zh", "c"))
    return jax.shard_map(
        body,
        mesh=fine,
        in_specs=(P(MODE, None, SPACE, None), P(None, SPACE, None), P()),
        out_specs=P(SPACE, MODE),
        check_vma=False,
    )
```

time: 82.8 us -> 81.6 us (0.986)
  Pallas kernels: 10.1 us -> 6.48 us
  blocking collectives: 56.9 us -> 59.4 us
    pallas_call x2, Pallas kernels: 8.88 us -> 5.28 us  [project(): pl.pallas_call(lambda *refs: kernel(*refs, rows=rows, edges=bool(edges)),...]
    all_to_all x1, blocking collectives: 33 us -> 35.5 us  [body(): shares = lax.all_to_all(shares, SPACE, 0, 0, tiled=True)]
  transfers between devices with their start and end apart: 2 -> 2, of which waited for: 0 -> 0; matrix products, arithmetic and copies ran while one was open for 0% -> 0% of each run, Pallas kernels for 5% -> 3%
where the time goes in v5:
time: 81.6 us; the launch traced here: 81.3 us
  blocking collectives  59.4 us (73%)
  starting transfers between devices  12.8 us (16%)
  Pallas kernels  6.48 us (8%)
  local copies, waits for them, and re-layouts  1.75 us (2%)
    all_to_all x1, blocking collectives, body(): shares = lax.all_to_all(shares, SPACE, 0, 0, tiled=True)  35.5 us
    all_to_all x1, blocking collectives, body(): pieces = lax.all_to_all(pack(plan.T, place, fields), MODE, 0, 0, tiled=True)  14 us
    all_to_all x1, blocking collectives, body(): recv = lax.all_to_all(choose(plan.T, place, pieces), MODE, 0, 0, tiled=True)  9.95 us
    ppermute x1, starting transfers between devices, body(): inner = lax.ppermute(inner, 'c', [(0, 1), (1, 0)])  7.12 us
    ppermute x1, starting transfers between devices, body(): outer = lax.ppermute(outer, SPACE, between)  5.72 us
    pallas_call x2, Pallas kernels, project(): pl.pallas_call(lambda *refs: kernel(*refs, rows=rows, edges=bool(edges)),...  5.28 us
  transfers between devices with their start and end apart: 2, of which 0 were waited for; matrix products, arithmetic and copies ran while one was open for 0% of the time, Pallas kernels for 3%

profile of v5, /device:TPU:1, one launch (start us, length us, event | category | flops | bytes accessed | tf_op | source)
XLA Modules:
  0.0 81.3 jit_solution(14744428544803426591)
XLA Ops:
  0.0 1.0 %copy.4 = bf16[8,8,2,4,256]{4,1,3,2,0:T(8,128)(2,1)S(1)} copy(bf16[8,8,2,4,256]{4,3,2,1,0:T(4,128)(2,1)} %bitcast.11) | data formatting | bytes 524288 | tf_op jit(solution)/shard_map/reshape | solution.py:171
  1.0 0.0 copy-start.1
  1.0 0.7 copy-done.1
  1.7 0.6 pack.1
  2.3 14.0 %all_to_all.15.pieces_ref = bf16[8,16,8,256]{3,2,1,0:T(8,128)(2,1)S(1)} all-to-all(bf16[8,16,8,256]{3,2,1,0:T(8,128)(2,1)S(1)} %pack.1), channel_id=1, replica_groups=mesh['x'=4,'zl'=2,'y'=8,'zh'=4,'c'=2] {'x','zl'}, dimensions={0} | all-to-all | bytes 1048576 | tf_op jit(solution)/shard_map/all_to_all | solution.py:173
  16.3 0.6 choose.1
  16.9 10.0 %all_to_all.16.recv_ref.refs_1_ = bf16[8,16,8,256]{3,2,1,0:T(8,128)(2,1)S(1)} all-to-all(bf16[8,16,8,256]{3,2,1,0:T(8,128)(2,1)S(1)} %choose.1), channel_id=1, replica_groups=mesh['x'=4,'zl'=2,'y'=8,'zh'=4,'c'=2] {'x','zl'}, dimensions={0} | all-to-all | bytes 1048576 | tf_op jit(solution)/shard_map/all_to_all | solution.py:174
  26.8 0.0 copy-start
  26.9 7.1 %collective-permute-start = (bf16[8,2,8,256]{3,2,1,0:T(8,128)(2,1)S(1)}, bf16[8,2,8,256]{3,2,1,0:T(8,128)(2,1)S(1)}, u32[]{:S(2)}, u32[]{:S(2)}) collective-permute-start(bf16[8,2,8,256]{3,2,1,0:T(8,128)(2,1)S(1)} %get-tuple-element.7), channel_id=1, source_target_pairs={{0,1},{1,0},{2,3},{3,2},{4,5},{5,4},{6,7},{7,6},{8,9},{9,8},{10,11... | collective-permute-start | bytes 196616 | tf_op jit(solution)/shard_map/ppermute | solution.py:179
  34.0 5.7 %collective-permute-start.1 = (bf16[8,2,8,256]{3,2,1,0:T(8,128)(2,1)S(1)}, bf16[8,2,8,256]{3,2,1,0:T(8,128)(2,1)S(1)}, u32[]{:S(2)}, u32[]{:S(2)}) collective-permute-start(bf16[8,2,8,256]{3,2,1,0:T(8,128)(2,1)S(1)} %get-tuple-element.8), channel_id=1, source_target_pairs={{1,2},{2,1},{3,4},{4,3},{5,6},{6,5},{7,8},{8,7},{9,10},{10,9},{11,... | collective-permute-start | bytes 196616 | tf_op jit(solution)/shard_map/ppermute | solution.py:178
  39.7 0.0 copy-done
  39.7 2.6 %project_middle.1.refs_6_ = f32[64,32,128]{2,1,0:T(8,128)S(1)} custom-call(f32[3,4,256]{2,1,0:T(4,128)S(1)} %copy-done, bf16[8,16,8,256]{3,2,1,0:T(8,128)(2,1)S(1)} %all_to_all.16.recv_ref.refs_1_, bf16[8,8,8,256]{3,2,1,0:T(8,128)(2,1)S(1)} %bitcast.7), custom_call_target="tpu_custom_call" | custom-call | tf_op jit(solution)/shard_map/project_middle/pallas_call | solution.py:149
  42.3 0.0 collective-permute-done.refs_4_
  42.3 0.0 collective-permute-done.1.refs_5_
  42.4 2.7 %project_edges.1 = bf16[64,32,128]{2,1,0:T(8,128)(2,1)S(1)} custom-call(f32[3,4,256]{2,1,0:T(4,128)S(1)} %copy-done, bf16[8,16,8,256]{3,2,1,0:T(8,128)(2,1)S(1)} %all_to_all.16.recv_ref.refs_1_, bf16[8,8,8,256]{3,2,1,0:T(8,128)(2,1)S(1)} %bitcast.8, s32[1]{0:T(128)} %bitcast.1.place_ref.refs_3_, bf16[8,2,8,256]{3,2,1,0:T(8,128)(2,1)S(1)} %collective-permute-done.refs_4_, ...), custom_call_target="tpu_custom_call" | custom-call | tf_op jit(solution)/shard_map/project_edges/pallas_call | solution.py:149
  45.0 35.5 %all_to_all.17 = bf16[64,32,128]{2,1,0:T(8,128)(2,1)S(1)} all-to-all(bf16[64,32,128]{2,1,0:T(8,128)(2,1)S(1)} %project_edges.1), channel_id=1, replica_groups=mesh['x'=4,'zl'=2,'y'=8,'zh'=4,'c'=2] {'y','zh','c'}, dimensions={0} | all-to-all | bytes 1048576 | tf_op jit(solution)/shard_map/all_to_all | solution.py:182
  80.5 0.1 convert_reduce_fusion
  80.6 0.1 fusion
  80.7 0.6 pad_maximum_fusion
  (2 shorter events, 0.0 us)
Async XLA Ops:
  1.0 0.7 copy-start.1
  26.8 12.9 %copy-start = (f32[3,4,256]{2,1,0:T(4,128)S(1)}, f32[3,4,256]{2,1,0:T(4,128)}, u32[]{:S(2)}) copy-start(f32[3,4,256]{2,1,0:T(4,128)} %refs_0_.3) | copy-start | bytes 36868
  26.9 15.5 %collective-permute-start = (bf16[8,2,8,256]{3,2,1,0:T(8,128)(2,1)S(1)}, bf16[8,2,8,256]{3,2,1,0:T(8,128)(2,1)S(1)}, u32[]{:S(2)}, u32[]{:S(2)}) collective-permute-start(bf16[8,2,8,256]{3,2,1,0:T(8,128)(2,1)S(1)} %get-tuple-element.7), channel_id=1, source_target_pairs={{0,1},{1,0},{2,3},{3,2},{4,5},{5,4},{6,7},{7,6},{8,9},{9,8},{10,11... | collective-permute-start | bytes 196616 | tf_op jit(solution)/shard_map/ppermute | solution.py:179
  34.0 8.4 %collective-permute-start.1 = (bf16[8,2,8,256]{3,2,1,0:T(8,128)(2,1)S(1)}, bf16[8,2,8,256]{3,2,1,0:T(8,128)(2,1)S(1)}, u32[]{:S(2)}, u32[]{:S(2)}) collective-permute-start(bf16[8,2,8,256]{3,2,1,0:T(8,128)(2,1)S(1)} %get-tuple-element.8), channel_id=1, source_target_pairs={{1,2},{2,1},{3,4},{4,3},{5,6},{6,5},{7,8},{8,7},{9,10},{10,9},{11,... | collective-permute-start | bytes 196616 | tf_op jit(solution)/shard_map/ppermute | solution.py:178

commit v6 on v5

--- a/solution.py
+++ b/solution.py
@@ -5,6 +5,7 @@
 from jax.experimental.pallas import tpu as pltpu
 from jax.sharding import Mesh, PartitionSpec as P
 
+
 MODE = ("x", "zl")
 SPACE = ("y", "zh", "c")
 JB = 8
@@ -15,7 +16,7 @@
 
 def pack_kernel(plan_ref, place_ref, fields_ref, out_ref):
     del place_ref
-    groups, _, m, ny = fields_ref.shape
+    groups, _, _, _ = fields_ref.shape
     half = groups // 2
     for b in range(2):
         mover = plan_ref[1, b] * half
@@ -78,11 +79,12 @@
     )(place, recv)
 
 
-def kernel(*refs, rows, edges):
+def kernel(*refs, rows, edges, send):
     metric_ref, recv_ref, test_ref, *refs = refs
     if edges:
         place_ref, inner_ref, outer_ref, acc_ref, *refs = refs
-        first = place_ref[0] % 2 == 0
+        core = place_ref[0] % 2
+        first = core == 0
     out_ref, s_ref, wm_ref, phi_ref, even_ref, odd_ref = refs
     groups, _, m, ny = recv_ref.shape
     n = groups * m
@@ -113,13 +115,18 @@
             wm_ref[at] = flat(recv_ref[:, 4 * c + r]) * metric_ref[2, pl.ds(r, 1), :]
             phi_ref[:, pl.ds(at * ny, ny)] = test_ref[:, 4 * c + r].reshape(n, ny)
 
+    pairs = n // 2
+    if edges:
+        side = 1 - core if send else core
+
     def build(block, f_ref):
         for at in range(2 * count):
             i = at % count
             s0 = s_ref[0, at]
             s1 = s_ref[1, at]
             for b in range(JB):
-                j = pl.ds(block * JB + b, 1)
+                slot = block * JB + b
+                j = pl.ds(2 * slot + side if edges else 2 * (slot % pairs) + slot // pairs, 1)
                 field = wm_ref[i, j, :] * s0 + wm_ref[count + i, j, :] * s1
                 f_ref[pl.ds(b * n, n), pl.ds(at * ny, ny)] = field.astype(jnp.bfloat16)
 
@@ -129,10 +136,10 @@
         res = jnp.concatenate([res[:, : n // 2], res[:, n // 2 :]], axis=2)
         here = pl.ds(block * JB, JB)
         if edges:
-            res = res + acc_ref[here]
+            res = res + acc_ref[pl.ds(side * pairs + block * JB, JB)]
         out_ref[here] = res.astype(out_ref.dtype)
 
-    blocks = n // JB
+    blocks = out_ref.shape[0] // JB
     buffers = (even_ref, odd_ref)
     build(0, even_ref)
     for block in range(blocks):
@@ -141,16 +148,16 @@
         multiply(block, buffers[block % 2])
 
 
-def project(metric, recv, test, rows, edges=None):
+def project(metric, recv, test, rows, edges=None, send=False):
     groups, _, m, ny = recv.shape
     n = groups * m
     width = 2 * len(rows)
     args = [metric, recv, test] + (edges or [])
     return pl.pallas_call(
-        lambda *refs: kernel(*refs, rows=rows, edges=bool(edges)),
+        lambda *refs: kernel(*refs, rows=rows, edges=bool(edges), send=send),
         in_specs=[VMEM] * 3 + ([SMEM] + [VMEM] * 3 if edges else []),
         out_specs=VMEM,
-        out_shape=jax.ShapeDtypeStruct((n, n // 2, 2 * n), jnp.bfloat16 if edges else jnp.float32),
+        out_shape=jax.ShapeDtypeStruct((n // 2 if edges else n, n // 2, 2 * n), jnp.float32),
         scratch_shapes=[
             pltpu.VMEM((2, width, n, ny), jnp.float32),
             pltpu.VMEM((width, n, ny), jnp.float32),
@@ -159,7 +166,7 @@
             pltpu.VMEM((JB * n, width * ny), jnp.bfloat16),
         ],
         compiler_params=pltpu.CompilerParams(vmem_limit_bytes=LIMIT),
-        name="project_edges" if edges else "project_middle",
+        name=("project_send" if send else "project_keep") if edges else "project_middle",
     )(*args)
 
 
@@ -178,8 +185,11 @@
     outer = lax.ppermute(outer, SPACE, between)
     inner = lax.ppermute(inner, "c", [(0, 1), (1, 0)])
     middle = project(metric, recv, fields, (1, 2))
-    shares = project(metric, recv, fields, (0, 3), [place, inner, outer, middle])
-    shares = lax.all_to_all(shares, SPACE, 0, 0, tiled=True)
+    edges = [place, inner, outer, middle]
+    sent = project(metric, recv, fields, (0, 3), edges, send=True)
+    other = lax.ppermute(sent, "c", [(0, 1), (1, 0)])
+    kept = project(metric, recv, fields, (0, 3), edges)
+    shares = lax.all_to_all((kept + other).astype(jnp.bfloat16), ("y", "zh"), 0, 0, tiled=True)
     norm_factor = float(4 * count * ny) ** (-0.5)
     total = jnp.sum(shares.astype(jnp.float32), axis=0) * norm_factor
     return jnp.concatenate([total[:, :n], total[:, n:]], axis=0)

time: 81.6 us -> 78.2 us (0.958)
  the two profiles are of different devices: /device:TPU:1 before, /device:TPU:8 now
where the time goes in v6:
time: 78.2 us; the launch traced here: 77.9 us
  blocking collectives  54.3 us (69%)
  starting transfers between devices  13.9 us (18%)
  Pallas kernels  6.69 us (9%)
  local copies, waits for them, and re-layouts  1.75 us (2%)
    all_to_all x1, blocking collectives, body(): lax.all_to_all((kept + other).astype(jnp.bfloat16), ('y', 'zh'), 0, 0, ti...  26.6 us
    all_to_all x1, blocking collectives, body(): pieces = lax.all_to_all(pack(plan.T, place, fields), MODE, 0, 0, tiled=True)  16 us
    all_to_all x1, blocking collectives, body(): recv = lax.all_to_all(choose(plan.T, place, pieces), MODE, 0, 0, tiled=True)  11.6 us
    ppermute x1, starting transfers between devices, body(): outer = lax.ppermute(outer, SPACE, between)  10 us
    pallas_call x3, Pallas kernels, project(): pl.pallas_call(lambda *refs: kernel(*refs, rows=rows, edges=bool(edges),...  5.5 us
    ppermute x1, starting transfers between devices, body(): other = lax.ppermute(sent, 'c', [(0, 1), (1, 0)])  1.92 us
    ppermute x1, starting transfers between devices, body(): inner = lax.ppermute(inner, 'c', [(0, 1), (1, 0)])  1.92 us
  transfers between devices with their start and end apart: 3, of which 1 were waited for; matrix products, arithmetic and copies ran while one was open for 0% of the time, Pallas kernels for 5%

profile of v6, /device:TPU:8, one launch (start us, length us, event | category | flops | bytes accessed | tf_op | source)
XLA Modules:
  0.0 77.9 jit_solution(2690273592356909874)
XLA Ops:
  0.0 1.0 %copy.4 = bf16[8,8,2,4,256]{4,1,3,2,0:T(8,128)(2,1)S(1)} copy(bf16[8,8,2,4,256]{4,3,2,1,0:T(4,128)(2,1)} %bitcast.12) | data formatting | bytes 524288 | tf_op jit(solution)/shard_map/reshape | solution.py:178
  1.0 0.0 copy-start.1
  1.0 0.7 copy-done.1
  1.7 0.6 pack.1
  2.3 16.0 %all_to_all.15.pieces_ref = bf16[8,16,8,256]{3,2,1,0:T(8,128)(2,1)S(1)} all-to-all(bf16[8,16,8,256]{3,2,1,0:T(8,128)(2,1)S(1)} %pack.1), channel_id=1, replica_groups=mesh['x'=4,'zl'=2,'y'=8,'zh'=4,'c'=2] {'x','zl'}, dimensions={0} | all-to-all | bytes 1048576 | tf_op jit(solution)/shard_map/all_to_all | solution.py:180
  18.3 0.6 choose.1
  18.9 11.6 %all_to_all.16.recv_ref.refs_1_ = bf16[8,16,8,256]{3,2,1,0:T(8,128)(2,1)S(1)} all-to-all(bf16[8,16,8,256]{3,2,1,0:T(8,128)(2,1)S(1)} %choose.1), channel_id=1, replica_groups=mesh['x'=4,'zl'=2,'y'=8,'zh'=4,'c'=2] {'x','zl'}, dimensions={0} | all-to-all | bytes 1048576 | tf_op jit(solution)/shard_map/all_to_all | solution.py:181
  30.6 0.0 copy-start
  30.6 1.9 %collective-permute-start = (bf16[8,2,8,256]{3,2,1,0:T(8,128)(2,1)S(1)}, bf16[8,2,8,256]{3,2,1,0:T(8,128)(2,1)S(1)}, u32[]{:S(2)}, u32[]{:S(2)}) collective-permute-start(bf16[8,2,8,256]{3,2,1,0:T(8,128)(2,1)S(1)} %get-tuple-element.7), channel_id=1, source_target_pairs={{0,1},{1,0},{2,3},{3,2},{4,5},{5,4},{6,7},{7,6},{8,9},{9,8},{10,11... | collective-permute-start | bytes 196616 | tf_op jit(solution)/shard_map/ppermute | solution.py:186
  32.5 10.0 %collective-permute-start.1 = (bf16[8,2,8,256]{3,2,1,0:T(8,128)(2,1)S(1)}, bf16[8,2,8,256]{3,2,1,0:T(8,128)(2,1)S(1)}, u32[]{:S(2)}, u32[]{:S(2)}) collective-permute-start(bf16[8,2,8,256]{3,2,1,0:T(8,128)(2,1)S(1)} %get-tuple-element.8), channel_id=1, source_target_pairs={{1,2},{2,1},{3,4},{4,3},{5,6},{6,5},{7,8},{8,7},{9,10},{10,9},{11,... | collective-permute-start | bytes 196616 | tf_op jit(solution)/shard_map/ppermute | solution.py:185
  42.6 0.0 copy-done
  42.6 2.6 %project_middle.1.refs_6_ = f32[64,32,128]{2,1,0:T(8,128)S(1)} custom-call(f32[3,4,256]{2,1,0:T(4,128)S(1)} %copy-done, bf16[8,16,8,256]{3,2,1,0:T(8,128)(2,1)S(1)} %all_to_all.16.recv_ref.refs_1_, bf16[8,8,8,256]{3,2,1,0:T(8,128)(2,1)S(1)} %bitcast.7), custom_call_target="tpu_custom_call" | custom-call | tf_op jit(solution)/shard_map/project_middle/pallas_call | solution.py:156
  45.2 0.0 collective-permute-done.refs_4_
  45.2 0.0 collective-permute-done.1.refs_5_
  45.2 1.5 %project_send.1 = f32[32,32,128]{2,1,0:T(8,128)S(1)} custom-call(f32[3,4,256]{2,1,0:T(4,128)S(1)} %copy-done, bf16[8,16,8,256]{3,2,1,0:T(8,128)(2,1)S(1)} %all_to_all.16.recv_ref.refs_1_, bf16[8,8,8,256]{3,2,1,0:T(8,128)(2,1)S(1)} %bitcast.8, s32[1]{0:T(128)} %bitcast.1.place_ref.refs_3_, bf16[8,2,8,256]{3,2,1,0:T(8,128)(2,1)S(1)} %collective-permute-done.refs_4_, ...), custom_call_target="tpu_custom_call" | custom-call | tf_op jit(solution)/shard_map/project_send/pallas_call | solution.py:156
  46.6 1.9 %collective-permute-start.2 = (f32[32,32,128]{2,1,0:T(8,128)S(1)}, f32[32,32,128]{2,1,0:T(8,128)S(1)}, u32[]{:S(2)}, u32[]{:S(2)}) collective-permute-start(f32[32,32,128]{2,1,0:T(8,128)S(1)} %project_send.1), channel_id=1, source_target_pairs={{0,1},{1,0},{2,3},{3,2},{4,5},{5,4},{6,7},{7,6},{8,9},{9,8},{10,11... | collective-permute-start | bytes 1572872 | tf_op jit(solution)/shard_map/ppermute | solution.py:190
  48.6 1.5 %project_keep.1 = f32[32,32,128]{2,1,0:T(8,128)S(1)} custom-call(f32[3,4,256]{2,1,0:T(4,128)S(1)} %copy-done, bf16[8,16,8,256]{3,2,1,0:T(8,128)(2,1)S(1)} %all_to_all.16.recv_ref.refs_1_, bf16[8,8,8,256]{3,2,1,0:T(8,128)(2,1)S(1)} %bitcast.9, s32[1]{0:T(128)} %bitcast.1.place_ref.refs_3_, bf16[8,2,8,256]{3,2,1,0:T(8,128)(2,1)S(1)} %collective-permute-done.refs_4_, ...), custom_call_target="tpu_custom_call" | custom-call | tf_op jit(solution)/shard_map/project_keep/pallas_call | solution.py:156
  50.0 0.4 collective-permute-done.2
  50.4 0.1 add_convert_fusion
  50.5 26.6 %all_to_all.17 = bf16[32,32,128]{2,1,0:T(8,128)(2,1)S(1)} all-to-all(bf16[32,32,128]{2,1,0:T(8,128)(2,1)S(1)} %add_convert_fusion), channel_id=1, replica_groups=mesh['x'=4,'zl'=2,'y'=8,'zh'=4,'c'=2] {'y','zh'}, dimensions={0} | all-to-all | bytes 524288 | tf_op jit(solution)/shard_map/all_to_all | solution.py:192
  77.2 0.1 fusion
  77.3 0.6 pad_maximum_fusion
  (3 shorter events, 0.1 us)
Async XLA Ops:
  1.0 0.7 copy-start.1
  30.6 12.0 %copy-start = (f32[3,4,256]{2,1,0:T(4,128)S(1)}, f32[3,4,256]{2,1,0:T(4,128)}, u32[]{:S(2)}) copy-start(f32[3,4,256]{2,1,0:T(4,128)} %refs_0_.5) | copy-start | bytes 36868
  30.6 14.6 %collective-permute-start = (bf16[8,2,8,256]{3,2,1,0:T(8,128)(2,1)S(1)}, bf16[8,2,8,256]{3,2,1,0:T(8,128)(2,1)S(1)}, u32[]{:S(2)}, u32[]{:S(2)}) collective-permute-start(bf16[8,2,8,256]{3,2,1,0:T(8,128)(2,1)S(1)} %get-tuple-element.7), channel_id=1, source_target_pairs={{0,1},{1,0},{2,3},{3,2},{4,5},{5,4},{6,7},{7,6},{8,9},{9,8},{10,11... | collective-permute-start | bytes 196616 | tf_op jit(solution)/shard_map/ppermute | solution.py:186
  32.5 12.7 %collective-permute-start.1 = (bf16[8,2,8,256]{3,2,1,0:T(8,128)(2,1)S(1)}, bf16[8,2,8,256]{3,2,1,0:T(8,128)(2,1)S(1)}, u32[]{:S(2)}, u32[]{:S(2)}) collective-permute-start(bf16[8,2,8,256]{3,2,1,0:T(8,128)(2,1)S(1)} %get-tuple-element.8), channel_id=1, source_target_pairs={{1,2},{2,1},{3,4},{4,3},{5,6},{6,5},{7,8},{8,7},{9,10},{10,9},{11,... | collective-permute-start | bytes 196616 | tf_op jit(solution)/shard_map/ppermute | solution.py:185
  46.6 3.8 %collective-permute-start.2 = (f32[32,32,128]{2,1,0:T(8,128)S(1)}, f32[32,32,128]{2,1,0:T(8,128)S(1)}, u32[]{:S(2)}, u32[]{:S(2)}) collective-permute-start(f32[32,32,128]{2,1,0:T(8,128)S(1)} %project_send.1), channel_id=1, source_target_pairs={{0,1},{1,0},{2,3},{3,2},{4,5},{5,4},{6,7},{7,6},{8,9},{9,8},{10,11... | collective-permute-start | bytes 1572872 | tf_op jit(solution)/shard_map/ppermute | solution.py:190

commit v7 on v6

--- a/solution.py
+++ b/solution.py
@@ -11,12 +11,22 @@
 JB = 8
 LIMIT = 16 * 2**20
 SMEM = pl.BlockSpec(memory_space=pltpu.SMEM)
+HBM = pl.BlockSpec(memory_space=pltpu.HBM)
 VMEM = pl.BlockSpec(memory_space=pltpu.VMEM)
 
 
-def pack_kernel(plan_ref, place_ref, fields_ref, out_ref):
-    del place_ref
-    groups, _, _, _ = fields_ref.shape
+def pack_kernel(plan_hbm, place_ref, raw_hbm, fields_ref, out_ref, pick_ref, plan_ref, raw_ref, sems):
+    raw_copy = pltpu.make_async_copy(raw_hbm, raw_ref, sems.at[0])
+    plan_copy = pltpu.make_async_copy(plan_hbm, plan_ref, sems.at[1])
+    raw_copy.start()
+    plan_copy.start()
+    raw_copy.wait()
+    groups, _, m, _ = fields_ref.shape
+    for g in range(groups):
+        for c in range(2):
+            block = raw_ref[g * m : (g + 1) * m, c].astype(jnp.float32)
+            fields_ref[g, 4 * c : 4 * c + 4] = jnp.swapaxes(block, 0, 1).astype(fields_ref.dtype)
+    plan_copy.wait()
     half = groups // 2
     for b in range(2):
         mover = plan_ref[1, b] * half
@@ -24,39 +34,52 @@
         for g in range(half):
             out_ref[b * half + g, 0:8] = fields_ref[mover + g]
             out_ref[b * half + g, 8:16] = fields_ref[moved + g]
-
-
-def pack(plan, place, fields):
-    groups, _, m, ny = fields.shape
+    block = place_ref[0] // groups
+    for kind in range(2):
+        owner = plan_ref[0, 2 * kind + block]
+        for g in range(groups):
+            pick_ref[kind, g] = jnp.full(pick_ref.shape[2:], jnp.where(owner == g, 1.0, 0.0), pick_ref.dtype)
+
+
+def pack(plan, place, mode_fields, groups):
+    modes, _, _, ny = mode_fields.shape
+    m = modes // groups
     return pl.pallas_call(
         pack_kernel,
-        in_specs=[SMEM, SMEM, VMEM],
-        out_specs=VMEM,
-        out_shape=jax.ShapeDtypeStruct((groups, 16, m, ny), fields.dtype),
+        in_specs=[HBM, SMEM, HBM],
+        out_specs=[VMEM, VMEM, VMEM],
+        out_shape=[
+            jax.ShapeDtypeStruct((groups, 8, m, ny), mode_fields.dtype),
+            jax.ShapeDtypeStruct((groups, 16, m, ny), mode_fields.dtype),
+            jax.ShapeDtypeStruct((2, groups, m, ny), jnp.float32),
+        ],
+        scratch_shapes=[
+            pltpu.SMEM(plan.shape, plan.dtype),
+            pltpu.VMEM(mode_fields.shape, mode_fields.dtype),
+            pltpu.SemaphoreType.DMA((2,)),
+        ],
         compiler_params=pltpu.CompilerParams(vmem_limit_bytes=LIMIT),
         name="pack",
-    )(plan, place, fields)
-
-
-def choose_kernel(plan_ref, place_ref, pieces_ref, out_ref):
+    )(plan, place, mode_fields)
+
+
+def choose_kernel(pick_ref, pieces_ref, out_ref):
     groups = pieces_ref.shape[0]
-    block = place_ref[0] // groups
-    mover = pieces_ref[plan_ref[0, block], 0:8]
-    moved = pieces_ref[plan_ref[0, 2 + block], 8:16]
-    for g in range(groups):
-        out_ref[g, 0:8] = mover
-        out_ref[g, 8:16] = moved
-
-
-def choose(plan, place, pieces):
+    for r in range(16):
+        piece = sum(pieces_ref[g, r].astype(jnp.float32) * pick_ref[r // 8, g] for g in range(groups))
+        for g in range(groups):
+            out_ref[g, r] = piece.astype(out_ref.dtype)
+
+
+def choose(pick, pieces):
     return pl.pallas_call(
         choose_kernel,
-        in_specs=[SMEM, SMEM, VMEM],
+        in_specs=[VMEM, VMEM],
         out_specs=VMEM,
         out_shape=jax.ShapeDtypeStruct(pieces.shape, pieces.dtype),
         compiler_params=pltpu.CompilerParams(vmem_limit_bytes=LIMIT),
         name="choose",
-    )(plan, place, pieces)
+    )(pick, pieces)
 
 
 def edge_kernel(place_ref, recv_ref, inner_ref, outer_ref):
@@ -174,11 +197,12 @@
     n = mode_fields.shape[0]
     ny = mode_fields.shape[3]
     groups = lax.axis_size(MODE)
-    m = n // groups
-    fields = mode_fields.reshape(groups, m, 2, 4, ny).transpose(0, 2, 3, 1, 4).reshape(groups, 8, m, ny)
     place = lax.axis_index(MODE + ("c",)).astype(jnp.int32).reshape(1)
-    pieces = lax.all_to_all(pack(plan.T, place, fields), MODE, 0, 0, tiled=True)
-    recv = lax.all_to_all(choose(plan.T, place, pieces), MODE, 0, 0, tiled=True)
+    plan = pltpu.with_memory_space_constraint(plan.T, pltpu.HBM)
+    raw = pltpu.with_memory_space_constraint(mode_fields, pltpu.HBM)
+    fields, packed, pick = pack(plan, place, raw, groups)
+    pieces = lax.all_to_all(packed, MODE, 0, 0, tiled=True)
+    recv = lax.all_to_all(choose(pick, pieces), MODE, 0, 0, tiled=True)
     count = lax.axis_size(SPACE)
     inner, outer = edge_rows(place, recv)
     between = [(i, i + 1 if i % 2 else i - 1) for i in range(1, count - 1)]

time: 78.2 us -> 76.6 us (0.980)
  local copies, waits for them, and re-layouts: 1.75 us -> 0.08 us
    reshape x1 -> x0, local copies, waits for them, and re-layouts: 1 us -> none  [body(): mode_fields.reshape(groups, m, 2, 4, ny).transpose(0, 2, 3, 1, 4)]
where the time goes in v7:
time: 76.6 us; the launch traced here: 76.2 us
  blocking collectives  54.3 us (71%)
  starting transfers between devices  13.9 us (18%)
  Pallas kernels  6.76 us (9%)
  other arithmetic  0.77 us (1%)
    all_to_all x1, blocking collectives, body(): lax.all_to_all((kept + other).astype(jnp.bfloat16), ('y', 'zh'), 0, 0, ti...  26.6 us
    all_to_all x1, blocking collectives, body(): pieces = lax.all_to_all(packed, MODE, 0, 0, tiled=True)  16 us
    all_to_all x1, blocking collectives, body(): recv = lax.all_to_all(choose(pick, pieces), MODE, 0, 0, tiled=True)  11.6 us
    ppermute x1, starting transfers between devices, body(): outer = lax.ppermute(outer, SPACE, between)  10 us
    pallas_call x3, Pallas kernels, project(): pl.pallas_call(lambda *refs: kernel(*refs, rows=rows, edges=bool(edges),...  5.49 us
    ppermute x1, starting transfers between devices, body(): other = lax.ppermute(sent, 'c', [(0, 1), (1, 0)])  1.92 us
    ppermute x1, starting transfers between devices, body(): inner = lax.ppermute(inner, 'c', [(0, 1), (1, 0)])  1.92 us
  transfers between devices with their start and end apart: 3, of which 1 were waited for; matrix products, arithmetic and copies ran while one was open for 0% of the time, Pallas kernels for 5%

profile of v7, /device:TPU:8, one launch (start us, length us, event | category | flops | bytes accessed | tf_op | source)
XLA Modules:
  0.0 76.2 jit_solution(16903963305430198955)
XLA Ops:
  0.0 1.1 %pack.1 = (bf16[8,8,8,256]{3,2,1,0:T(8,128)(2,1)S(1)}, bf16[8,16,8,256]{3,2,1,0:T(8,128)(2,1)S(1)}, f32[2,8,8,256]{3,2,1,0:T(8,128)S(1)}) custom-call(s32[2,4]{1,0:T(2,128)} %bitcast.2, s32[1]{0:T(128)} %bitcast.1.place_ref.refs_3_, bf16[64,2,4,256]{3,2,1,0:T(4,128)(2,1)} %raw_hbm.1), custom_call_target="tpu_custom_call" | custom-call | tf_op jit(solution)/shard_map/pack/pallas_call | solution.py:47
  1.1 16.0 %all_to_all.15.pieces_ref = bf16[8,16,8,256]{3,2,1,0:T(8,128)(2,1)S(1)} all-to-all(bf16[8,16,8,256]{3,2,1,0:T(8,128)(2,1)S(1)} %get-tuple-element.11), channel_id=1, replica_groups=mesh['x'=4,'zl'=2,'y'=8,'zh'=4,'c'=2] {'x','zl'}, dimensions={0} | all-to-all | bytes 1048576 | tf_op jit(solution)/shard_map/all_to_all | solution.py:204
  17.2 0.1 choose.1
  17.3 11.6 %all_to_all.16.recv_ref.refs_1_ = bf16[8,16,8,256]{3,2,1,0:T(8,128)(2,1)S(1)} all-to-all(bf16[8,16,8,256]{3,2,1,0:T(8,128)(2,1)S(1)} %choose.1), channel_id=1, replica_groups=mesh['x'=4,'zl'=2,'y'=8,'zh'=4,'c'=2] {'x','zl'}, dimensions={0} | all-to-all | bytes 1048576 | tf_op jit(solution)/shard_map/all_to_all | solution.py:205
  28.9 0.0 copy-start
  28.9 1.9 %collective-permute-start = (bf16[8,2,8,256]{3,2,1,0:T(8,128)(2,1)S(1)}, bf16[8,2,8,256]{3,2,1,0:T(8,128)(2,1)S(1)}, u32[]{:S(2)}, u32[]{:S(2)}) collective-permute-start(bf16[8,2,8,256]{3,2,1,0:T(8,128)(2,1)S(1)} %get-tuple-element.13), channel_id=1, source_target_pairs={{0,1},{1,0},{2,3},{3,2},{4,5},{5,4},{6,7},{7,6},{8,9},{9,8},{10,11... | collective-permute-start | bytes 196616 | tf_op jit(solution)/shard_map/ppermute | solution.py:210
  30.9 10.0 %collective-permute-start.1 = (bf16[8,2,8,256]{3,2,1,0:T(8,128)(2,1)S(1)}, bf16[8,2,8,256]{3,2,1,0:T(8,128)(2,1)S(1)}, u32[]{:S(2)}, u32[]{:S(2)}) collective-permute-start(bf16[8,2,8,256]{3,2,1,0:T(8,128)(2,1)S(1)} %get-tuple-element.14), channel_id=1, source_target_pairs={{1,2},{2,1},{3,4},{4,3},{5,6},{6,5},{7,8},{8,7},{9,10},{10,9},{11,... | collective-permute-start | bytes 196616 | tf_op jit(solution)/shard_map/ppermute | solution.py:209
  40.9 0.0 copy-done
  40.9 2.6 %project_middle.1.refs_6_ = f32[64,32,128]{2,1,0:T(8,128)S(1)} custom-call(f32[3,4,256]{2,1,0:T(4,128)S(1)} %copy-done, bf16[8,16,8,256]{3,2,1,0:T(8,128)(2,1)S(1)} %all_to_all.16.recv_ref.refs_1_, bf16[8,8,8,256]{3,2,1,0:T(8,128)(2,1)S(1)} %get-tuple-element.12.refs_2_), custom_call_target="tpu_custom_call" | custom-call | tf_op jit(solution)/shard_map/project_middle/pallas_call | solution.py:179
  43.5 0.0 collective-permute-done.refs_4_
  43.5 0.0 collective-permute-done.1.refs_5_
  43.5 1.5 %project_send.1 = f32[32,32,128]{2,1,0:T(8,128)S(1)} custom-call(f32[3,4,256]{2,1,0:T(4,128)S(1)} %copy-done, bf16[8,16,8,256]{3,2,1,0:T(8,128)(2,1)S(1)} %all_to_all.16.recv_ref.refs_1_, bf16[8,8,8,256]{3,2,1,0:T(8,128)(2,1)S(1)} %get-tuple-element.12.refs_2_, s32[1]{0:T(128)} %bitcast.1.place_ref.refs_3_, ...), custom_call_target="tpu_custom_call" | custom-call | tf_op jit(solution)/shard_map/project_send/pallas_call | solution.py:179
  45.0 1.9 %collective-permute-start.2 = (f32[32,32,128]{2,1,0:T(8,128)S(1)}, f32[32,32,128]{2,1,0:T(8,128)S(1)}, u32[]{:S(2)}, u32[]{:S(2)}) collective-permute-start(f32[32,32,128]{2,1,0:T(8,128)S(1)} %project_send.1), channel_id=1, source_target_pairs={{0,1},{1,0},{2,3},{3,2},{4,5},{5,4},{6,7},{7,6},{8,9},{9,8},{10,11... | collective-permute-start | bytes 1572872 | tf_op jit(solution)/shard_map/ppermute | solution.py:214
  46.9 1.5 %project_keep.1 = f32[32,32,128]{2,1,0:T(8,128)S(1)} custom-call(f32[3,4,256]{2,1,0:T(4,128)S(1)} %copy-done, bf16[8,16,8,256]{3,2,1,0:T(8,128)(2,1)S(1)} %all_to_all.16.recv_ref.refs_1_, bf16[8,8,8,256]{3,2,1,0:T(8,128)(2,1)S(1)} %get-tuple-element.12.refs_2_, s32[1]{0:T(128)} %bitcast.1.place_ref.refs_3_, ...), custom_call_target="tpu_custom_call" | custom-call | tf_op jit(solution)/shard_map/project_keep/pallas_call | solution.py:179
  48.4 0.4 collective-permute-done.2
  48.8 0.1 add_convert_fusion
  48.9 26.6 %all_to_all.17 = bf16[32,32,128]{2,1,0:T(8,128)(2,1)S(1)} all-to-all(bf16[32,32,128]{2,1,0:T(8,128)(2,1)S(1)} %add_convert_fusion), channel_id=1, replica_groups=mesh['x'=4,'zl'=2,'y'=8,'zh'=4,'c'=2] {'y','zh'}, dimensions={0} | all-to-all | bytes 524288 | tf_op jit(solution)/shard_map/all_to_all | solution.py:216
  75.5 0.1 fusion
  75.6 0.6 pad_maximum_fusion
  (3 shorter events, 0.1 us)
Async XLA Ops:
  28.9 12.0 %copy-start = (f32[3,4,256]{2,1,0:T(4,128)S(1)}, f32[3,4,256]{2,1,0:T(4,128)}, u32[]{:S(2)}) copy-start(f32[3,4,256]{2,1,0:T(4,128)} %refs_0_.5) | copy-start | bytes 36868
  28.9 14.6 %collective-permute-start = (bf16[8,2,8,256]{3,2,1,0:T(8,128)(2,1)S(1)}, bf16[8,2,8,256]{3,2,1,0:T(8,128)(2,1)S(1)}, u32[]{:S(2)}, u32[]{:S(2)}) collective-permute-start(bf16[8,2,8,256]{3,2,1,0:T(8,128)(2,1)S(1)} %get-tuple-element.13), channel_id=1, source_target_pairs={{0,1},{1,0},{2,3},{3,2},{4,5},{5,4},{6,7},{7,6},{8,9},{9,8},{10,11... | collective-permute-start | bytes 196616 | tf_op jit(solution)/shard_map/ppermute | solution.py:210
  30.9 12.6 %collective-permute-start.1 = (bf16[8,2,8,256]{3,2,1,0:T(8,128)(2,1)S(1)}, bf16[8,2,8,256]{3,2,1,0:T(8,128)(2,1)S(1)}, u32[]{:S(2)}, u32[]{:S(2)}) collective-permute-start(bf16[8,2,8,256]{3,2,1,0:T(8,128)(2,1)S(1)} %get-tuple-element.14), channel_id=1, source_target_pairs={{1,2},{2,1},{3,4},{4,3},{5,6},{6,5},{7,8},{8,7},{9,10},{10,9},{11,... | collective-permute-start | bytes 196616 | tf_op jit(solution)/shard_map/ppermute | solution.py:209
  45.0 3.8 %collective-permute-start.2 = (f32[32,32,128]{2,1,0:T(8,128)S(1)}, f32[32,32,128]{2,1,0:T(8,128)S(1)}, u32[]{:S(2)}, u32[]{:S(2)}) collective-permute-start(f32[32,32,128]{2,1,0:T(8,128)S(1)} %project_send.1), channel_id=1, source_target_pairs={{0,1},{1,0},{2,3},{3,2},{4,5},{5,4},{6,7},{7,6},{8,9},{9,8},{10,11... | collective-permute-start | bytes 1572872 | tf_op jit(solution)/shard_map/ppermute | solution.py:214

commit v8 on v7

--- a/solution.py
+++ b/solution.py
@@ -8,7 +8,7 @@
 
 MODE = ("x", "zl")
 SPACE = ("y", "zh", "c")
-JB = 8
+JB = 4
 LIMIT = 16 * 2**20
 SMEM = pl.BlockSpec(memory_space=pltpu.SMEM)
 HBM = pl.BlockSpec(memory_space=pltpu.HBM)
@@ -102,12 +102,14 @@
     )(place, recv)
 
 
-def kernel(*refs, rows, edges, send):
-    metric_ref, recv_ref, test_ref, *refs = refs
+def kernel(*refs, rows, edges, more, send):
+    metric_ref, recv_ref, test_ref, place_ref, *refs = refs
+    core = place_ref[0] % 2
     if edges:
-        place_ref, inner_ref, outer_ref, acc_ref, *refs = refs
-        core = place_ref[0] % 2
         first = core == 0
+        inner_ref, outer_ref, *refs = refs
+    if more:
+        acc_ref, *refs = refs
     out_ref, s_ref, wm_ref, phi_ref, even_ref, odd_ref = refs
     groups, _, m, ny = recv_ref.shape
     n = groups * m
@@ -138,9 +140,7 @@
             wm_ref[at] = flat(recv_ref[:, 4 * c + r]) * metric_ref[2, pl.ds(r, 1), :]
             phi_ref[:, pl.ds(at * ny, ny)] = test_ref[:, 4 * c + r].reshape(n, ny)
 
-    pairs = n // 2
-    if edges:
-        side = 1 - core if send else core
+    side = 1 - core if send else core
 
     def build(block, f_ref):
         for at in range(2 * count):
@@ -149,7 +149,7 @@
             s1 = s_ref[1, at]
             for b in range(JB):
                 slot = block * JB + b
-                j = pl.ds(2 * slot + side if edges else 2 * (slot % pairs) + slot // pairs, 1)
+                j = pl.ds(2 * slot + side, 1)
                 field = wm_ref[i, j, :] * s0 + wm_ref[count + i, j, :] * s1
                 f_ref[pl.ds(b * n, n), pl.ds(at * ny, ny)] = field.astype(jnp.bfloat16)
 
@@ -158,8 +158,8 @@
         res = res.reshape(JB, n, n)
         res = jnp.concatenate([res[:, : n // 2], res[:, n // 2 :]], axis=2)
         here = pl.ds(block * JB, JB)
-        if edges:
-            res = res + acc_ref[pl.ds(side * pairs + block * JB, JB)]
+        if more:
+            res = res + acc_ref[here]
         out_ref[here] = res.astype(out_ref.dtype)
 
     blocks = out_ref.shape[0] // JB
@@ -171,16 +171,16 @@
         multiply(block, buffers[block % 2])
 
 
-def project(metric, recv, test, rows, edges=None, send=False):
+def project(metric, recv, test, place, rows, edges=(), acc=(), send=False):
     groups, _, m, ny = recv.shape
     n = groups * m
     width = 2 * len(rows)
-    args = [metric, recv, test] + (edges or [])
-    return pl.pallas_call(
-        lambda *refs: kernel(*refs, rows=rows, edges=bool(edges), send=send),
-        in_specs=[VMEM] * 3 + ([SMEM] + [VMEM] * 3 if edges else []),
+    args = [metric, recv, test, place, *edges, *acc]
+    return pl.pallas_call(
+        lambda *refs: kernel(*refs, rows=rows, edges=bool(edges), more=bool(acc), send=send),
+        in_specs=[VMEM] * 3 + [SMEM] + [VMEM] * (len(args) - 4),
         out_specs=VMEM,
-        out_shape=jax.ShapeDtypeStruct((n // 2 if edges else n, n // 2, 2 * n), jnp.float32),
+        out_shape=jax.ShapeDtypeStruct((n // 2, n // 2, 2 * n), jnp.float32),
         scratch_shapes=[
             pltpu.VMEM((2, width, n, ny), jnp.float32),
             pltpu.VMEM((width, n, ny), jnp.float32),
@@ -189,12 +189,28 @@
             pltpu.VMEM((JB * n, width * ny), jnp.bfloat16),
         ],
         compiler_params=pltpu.CompilerParams(vmem_limit_bytes=LIMIT),
-        name=("project_send" if send else "project_keep") if edges else "project_middle",
     )(*args)
 
 
+def finish_kernel(shares_ref, out_ref, *, factor):
+    count, _, width = shares_ref.shape
+    total = sum(shares_ref[q].astype(jnp.float32) for q in range(count)) * factor
+    out_ref[...] = jnp.concatenate([total[:, : width // 2], total[:, width // 2 :]], axis=0)
+
+
+def finish(shares, factor):
+    _, half, width = shares.shape
+    return pl.pallas_call(
+        lambda *refs: finish_kernel(*refs, factor=factor),
+        in_specs=[VMEM],
+        out_specs=VMEM,
+        out_shape=jax.ShapeDtypeStruct((2 * half, width // 2), jnp.float32),
+        compiler_params=pltpu.CompilerParams(vmem_limit_bytes=LIMIT),
+        name="finish",
+    )(shares)
+
+
 def body(mode_fields, metric, plan):
-    n = mode_fields.shape[0]
     ny = mode_fields.shape[3]
     groups = lax.axis_size(MODE)
     place = lax.axis_index(MODE + ("c",)).astype(jnp.int32).reshape(1)
@@ -208,15 +224,13 @@
     between = [(i, i + 1 if i % 2 else i - 1) for i in range(1, count - 1)]
     outer = lax.ppermute(outer, SPACE, between)
     inner = lax.ppermute(inner, "c", [(0, 1), (1, 0)])
-    middle = project(metric, recv, fields, (1, 2))
-    edges = [place, inner, outer, middle]
-    sent = project(metric, recv, fields, (0, 3), edges, send=True)
+    edges = (inner, outer)
+    middle = project(metric, recv, fields, place, (1, 2), send=True)
+    sent = project(metric, recv, fields, place, (0, 3), edges, (middle,), send=True)
     other = lax.ppermute(sent, "c", [(0, 1), (1, 0)])
-    kept = project(metric, recv, fields, (0, 3), edges)
+    kept = project(metric, recv, fields, place, (0, 1, 2, 3), edges)
     shares = lax.all_to_all((kept + other).astype(jnp.bfloat16), ("y", "zh"), 0, 0, tiled=True)
-    norm_factor = float(4 * count * ny) ** (-0.5)
-    total = jnp.sum(shares.astype(jnp.float32), axis=0) * norm_factor
-    return jnp.concatenate([total[:, :n], total[:, n:]], axis=0)
+    return finish(shares, float(4 * count * ny) ** (-0.5))
 
 
 def solution(mesh):

time: 76.6 us -> 77.5 us (1.012)
  Pallas kernels: 6.76 us -> 7.69 us
where the time goes in v8:
time: 77.5 us; the launch traced here: 77.2 us
  blocking collectives  54.9 us (71%)
  starting transfers between devices  13.9 us (18%)
  Pallas kernels  7.69 us (10%)
    all_to_all x1, blocking collectives, body(): lax.all_to_all((kept + other).astype(jnp.bfloat16), ('y', 'zh'), 0, 0, ti...  27.2 us
    all_to_all x1, blocking collectives, body(): pieces = lax.all_to_all(packed, MODE, 0, 0, tiled=True)  16 us
    all_to_all x1, blocking collectives, body(): recv = lax.all_to_all(choose(pick, pieces), MODE, 0, 0, tiled=True)  11.6 us
    ppermute x1, starting transfers between devices, body(): outer = lax.ppermute(outer, SPACE, between)  10 us
    pallas_call x3, Pallas kernels, project(): pl.pallas_call(lambda *refs: kernel(*refs, rows=rows, edges=bool(edges),...  5.69 us
    ppermute x1, starting transfers between devices, body(): other = lax.ppermute(sent, 'c', [(0, 1), (1, 0)])  1.92 us
    ppermute x1, starting transfers between devices, body(): inner = lax.ppermute(inner, 'c', [(0, 1), (1, 0)])  1.92 us
  transfers between devices with their start and end apart: 3, of which 1 were waited for; matrix products, arithmetic and copies ran while one was open for 0% of the time, Pallas kernels for 5%

profile of v8, /device:TPU:8, one launch (start us, length us, event | category | flops | bytes accessed | tf_op | source)
XLA Modules:
  0.0 77.2 jit_solution(4396372750264839144)
XLA Ops:
  0.0 1.1 %pack.1 = (bf16[8,8,8,256]{3,2,1,0:T(8,128)(2,1)S(1)}, bf16[8,16,8,256]{3,2,1,0:T(8,128)(2,1)S(1)}, f32[2,8,8,256]{3,2,1,0:T(8,128)S(1)}) custom-call(s32[2,4]{1,0:T(2,128)} %bitcast.2, s32[1]{0:T(128)} %bitcast.1.place_ref.refs_3_, bf16[64,2,4,256]{3,2,1,0:T(4,128)(2,1)} %raw_hbm.1), custom_call_target="tpu_custom_call" | custom-call | tf_op jit(solution)/shard_map/pack/pallas_call | solution.py:47
  1.1 16.0 %all_to_all.15.pieces_ref = bf16[8,16,8,256]{3,2,1,0:T(8,128)(2,1)S(1)} all-to-all(bf16[8,16,8,256]{3,2,1,0:T(8,128)(2,1)S(1)} %get-tuple-element.11), channel_id=1, replica_groups=mesh['x'=4,'zl'=2,'y'=8,'zh'=4,'c'=2] {'x','zl'}, dimensions={0} | all-to-all | bytes 1048576 | tf_op jit(solution)/shard_map/all_to_all | solution.py:220
  17.2 0.1 choose.1
  17.3 11.6 %all_to_all.16.recv_ref.refs_1_ = bf16[8,16,8,256]{3,2,1,0:T(8,128)(2,1)S(1)} all-to-all(bf16[8,16,8,256]{3,2,1,0:T(8,128)(2,1)S(1)} %choose.1), channel_id=1, replica_groups=mesh['x'=4,'zl'=2,'y'=8,'zh'=4,'c'=2] {'x','zl'}, dimensions={0} | all-to-all | bytes 1048576 | tf_op jit(solution)/shard_map/all_to_all | solution.py:221
  28.9 0.0 copy-start
  29.0 1.9 %collective-permute-start = (bf16[8,2,8,256]{3,2,1,0:T(8,128)(2,1)S(1)}, bf16[8,2,8,256]{3,2,1,0:T(8,128)(2,1)S(1)}, u32[]{:S(2)}, u32[]{:S(2)}) collective-permute-start(bf16[8,2,8,256]{3,2,1,0:T(8,128)(2,1)S(1)} %get-tuple-element.13), channel_id=1, source_target_pairs={{0,1},{1,0},{2,3},{3,2},{4,5},{5,4},{6,7},{7,6},{8,9},{9,8},{10,11... | collective-permute-start | bytes 196616 | tf_op jit(solution)/shard_map/ppermute | solution.py:226
  30.9 10.0 %collective-permute-start.1 = (bf16[8,2,8,256]{3,2,1,0:T(8,128)(2,1)S(1)}, bf16[8,2,8,256]{3,2,1,0:T(8,128)(2,1)S(1)}, u32[]{:S(2)}, u32[]{:S(2)}) collective-permute-start(bf16[8,2,8,256]{3,2,1,0:T(8,128)(2,1)S(1)} %get-tuple-element.14), channel_id=1, source_target_pairs={{1,2},{2,1},{3,4},{4,3},{5,6},{6,5},{7,8},{8,7},{9,10},{10,9},{11,... | collective-permute-start | bytes 196616 | tf_op jit(solution)/shard_map/ppermute | solution.py:225
  40.9 0.0 copy-done
  40.9 1.5 %shard_map.38.refs_6_ = f32[32,32,128]{2,1,0:T(8,128)S(1)} custom-call(f32[3,4,256]{2,1,0:T(4,128)S(1)} %copy-done, bf16[8,16,8,256]{3,2,1,0:T(8,128)(2,1)S(1)} %all_to_all.16.recv_ref.refs_1_, bf16[8,8,8,256]{3,2,1,0:T(8,128)(2,1)S(1)} %get-tuple-element.12.refs_2_, s32[1]{0:T(128)} %bitcast.1.place_ref.refs_3_), custom_call_target="tpu_custom_call" | custom-call | tf_op jit(solution)/shard_map/pallas_call | solution.py:179
  42.4 0.0 collective-permute-done.refs_4_
  42.4 0.5 collective-permute-done.1.refs_5_
  42.9 1.5 %shard_map.39 = f32[32,32,128]{2,1,0:T(8,128)S(1)} custom-call(f32[3,4,256]{2,1,0:T(4,128)S(1)} %copy-done, bf16[8,16,8,256]{3,2,1,0:T(8,128)(2,1)S(1)} %all_to_all.16.recv_ref.refs_1_, bf16[8,8,8,256]{3,2,1,0:T(8,128)(2,1)S(1)} %get-tuple-element.12.refs_2_, s32[1]{0:T(128)} %bitcast.1.place_ref.refs_3_, ...), custom_call_target="tpu_custom_call" | custom-call | tf_op jit(solution)/shard_map/pallas_call | solution.py:179
  44.4 1.9 %collective-permute-start.2 = (f32[32,32,128]{2,1,0:T(8,128)S(1)}, f32[32,32,128]{2,1,0:T(8,128)S(1)}, u32[]{:S(2)}, u32[]{:S(2)}) collective-permute-start(f32[32,32,128]{2,1,0:T(8,128)S(1)} %shard_map.39), channel_id=1, source_target_pairs={{0,1},{1,0},{2,3},{3,2},{4,5},{5,4},{6,7},{7,6},{8,9},{9,8},{10,11... | collective-permute-start | bytes 1572872 | tf_op jit(solution)/shard_map/ppermute | solution.py:230
  46.4 2.8 %shard_map.37 = f32[32,32,128]{2,1,0:T(8,128)S(1)} custom-call(f32[3,4,256]{2,1,0:T(4,128)S(1)} %copy-done, bf16[8,16,8,256]{3,2,1,0:T(8,128)(2,1)S(1)} %all_to_all.16.recv_ref.refs_1_, bf16[8,8,8,256]{3,2,1,0:T(8,128)(2,1)S(1)} %get-tuple-element.12.refs_2_, s32[1]{0:T(128)} %bitcast.1.place_ref.refs_3_, ...), custom_call_target="tpu_custom_call" | custom-call | tf_op jit(solution)/shard_map/pallas_call | solution.py:179
  49.1 0.0 collective-permute-done.2
  49.1 0.1 add_convert_fusion
  49.2 27.2 %all_to_all.17.refs_0_ = bf16[32,32,128]{2,1,0:T(8,128)(2,1)S(1)} all-to-all(bf16[32,32,128]{2,1,0:T(8,128)(2,1)S(1)} %add_convert_fusion), channel_id=1, replica_groups=mesh['x'=4,'zl'=2,'y'=8,'zh'=4,'c'=2] {'y','zh'}, dimensions={0} | all-to-all | bytes 524288 | tf_op jit(solution)/shard_map/all_to_all | solution.py:232
  76.4 0.7 finish.1
  (1 shorter events, 0.0 us)
Async XLA Ops:
  28.9 12.0 %copy-start = (f32[3,4,256]{2,1,0:T(4,128)S(1)}, f32[3,4,256]{2,1,0:T(4,128)}, u32[]{:S(2)}) copy-start(f32[3,4,256]{2,1,0:T(4,128)} %refs_0_.5) | copy-start | bytes 36868
  29.0 13.4 %collective-permute-start = (bf16[8,2,8,256]{3,2,1,0:T(8,128)(2,1)S(1)}, bf16[8,2,8,256]{3,2,1,0:T(8,128)(2,1)S(1)}, u32[]{:S(2)}, u32[]{:S(2)}) collective-permute-start(bf16[8,2,8,256]{3,2,1,0:T(8,128)(2,1)S(1)} %get-tuple-element.13), channel_id=1, source_target_pairs={{0,1},{1,0},{2,3},{3,2},{4,5},{5,4},{6,7},{7,6},{8,9},{9,8},{10,11... | collective-permute-start | bytes 196616 | tf_op jit(solution)/shard_map/ppermute | solution.py:226
  30.9 12.1 %collective-permute-start.1 = (bf16[8,2,8,256]{3,2,1,0:T(8,128)(2,1)S(1)}, bf16[8,2,8,256]{3,2,1,0:T(8,128)(2,1)S(1)}, u32[]{:S(2)}, u32[]{:S(2)}) collective-permute-start(bf16[8,2,8,256]{3,2,1,0:T(8,128)(2,1)S(1)} %get-tuple-element.14), channel_id=1, source_target_pairs={{1,2},{2,1},{3,4},{4,3},{5,6},{6,5},{7,8},{8,7},{9,10},{10,9},{11,... | collective-permute-start | bytes 196616 | tf_op jit(solution)/shard_map/ppermute | solution.py:225
  44.4 4.7 %collective-permute-start.2 = (f32[32,32,128]{2,1,0:T(8,128)S(1)}, f32[32,32,128]{2,1,0:T(8,128)S(1)}, u32[]{:S(2)}, u32[]{:S(2)}) collective-permute-start(f32[32,32,128]{2,1,0:T(8,128)S(1)} %shard_map.39), channel_id=1, source_target_pairs={{0,1},{1,0},{2,3},{3,2},{4,5},{5,4},{6,7},{7,6},{8,9},{9,8},{10,11... | collective-permute-start | bytes 1572872 | tf_op jit(solution)/shard_map/ppermute | solution.py:230

commit v9 on v8

--- a/solution.py
+++ b/solution.py
@@ -7,6 +7,7 @@
 
 
 MODE = ("x", "zl")
+RING = ("zl", "x")
 SPACE = ("y", "zh", "c")
 JB = 4
 LIMIT = 16 * 2**20
@@ -37,6 +38,7 @@
     block = place_ref[0] // groups
     for kind in range(2):
         owner = plan_ref[0, 2 * kind + block]
+        owner = owner % 2 * half + owner // 2
         for g in range(groups):
             pick_ref[kind, g] = jnp.full(pick_ref.shape[2:], jnp.where(owner == g, 1.0, 0.0), pick_ref.dtype)
 
@@ -212,20 +214,21 @@
 
 def body(mode_fields, metric, plan):
     ny = mode_fields.shape[3]
-    groups = lax.axis_size(MODE)
-    place = lax.axis_index(MODE + ("c",)).astype(jnp.int32).reshape(1)
+    groups = lax.axis_size(RING)
+    place = lax.axis_index(RING + ("c",)).astype(jnp.int32).reshape(1)
     plan = pltpu.with_memory_space_constraint(plan.T, pltpu.HBM)
     raw = pltpu.with_memory_space_constraint(mode_fields, pltpu.HBM)
     fields, packed, pick = pack(plan, place, raw, groups)
-    pieces = lax.all_to_all(packed, MODE, 0, 0, tiled=True)
-    recv = lax.all_to_all(choose(pick, pieces), MODE, 0, 0, tiled=True)
+    pieces = lax.all_to_all(packed, RING, 0, 0, tiled=True)
+    recv = lax.all_to_all(choose(pick, pieces), RING, 0, 0, tiled=True)
     count = lax.axis_size(SPACE)
     inner, outer = edge_rows(place, recv)
     between = [(i, i + 1 if i % 2 else i - 1) for i in range(1, count - 1)]
     outer = lax.ppermute(outer, SPACE, between)
+    middle = project(metric, recv, fields, place, (1, 2), send=True)
+    inner, middle = lax.optimization_barrier((inner, middle))
     inner = lax.ppermute(inner, "c", [(0, 1), (1, 0)])
     edges = (inner, outer)
-    middle = project(metric, recv, fields, place, (1, 2), send=True)
     sent = project(metric, recv, fields, place, (0, 3), edges, (middle,), send=True)
     other = lax.ppermute(sent, "c", [(0, 1), (1, 0)])
     kept = project(metric, recv, fields, place, (0, 1, 2, 3), edges)

time: 77.5 us -> 75 us (0.968)
  starting transfers between devices: 13.9 us -> 10.6 us
    ppermute x1, starting transfers between devices: 10 us -> 6.65 us  [body(): outer = lax.ppermute(outer, SPACE, between)]
    ppermute x1, waiting for transfers between devices: 0.01 us -> 1.21 us  [body(): inner = lax.ppermute(inner, 'c', [(0, 1), (1, 0)])]
  transfers between devices with their start and end apart: 3 -> 3, of which waited for: 1 -> 1; matrix products, arithmetic and copies ran while one was open for 0% -> 0% of each run, Pallas kernels for 5% -> 6%
where the time goes in v9:
time: 75 us; the launch traced here: 74.6 us
  blocking collectives  54.9 us (73%)
  starting transfers between devices  10.6 us (14%)
  Pallas kernels  7.68 us (10%)
  waiting for transfers between devices  1.21 us (2%)
    all_to_all x1, blocking collectives, body(): lax.all_to_all((kept + other).astype(jnp.bfloat16), ('y', 'zh'), 0, 0, ti...  27.5 us
    all_to_all x1, blocking collectives, body(): pieces = lax.all_to_all(packed, RING, 0, 0, tiled=True)  16 us
    all_to_all x1, blocking collectives, body(): recv = lax.all_to_all(choose(pick, pieces), RING, 0, 0, tiled=True)  11.4 us
    ppermute x1, starting transfers between devices, body(): outer = lax.ppermute(outer, SPACE, between)  6.65 us
    pallas_call x3, Pallas kernels, project(): pl.pallas_call(lambda *refs: kernel(*refs, rows=rows, edges=bool(edges),...  5.68 us
    ppermute x1, starting transfers between devices, body(): other = lax.ppermute(sent, 'c', [(0, 1), (1, 0)])  2.07 us
    ppermute x1, starting transfers between devices, body(): inner = lax.ppermute(inner, 'c', [(0, 1), (1, 0)])  1.92 us
  transfers between devices with their start and end apart: 3, of which 1 were waited for; matrix products, arithmetic and copies ran while one was open for 0% of the time, Pallas kernels for 6%

profile of v9, /device:TPU:8, one launch (start us, length us, event | category | flops | bytes accessed | tf_op | source)
XLA Modules:
  0.0 74.6 jit_solution(11782836218177558422)
XLA Ops:
  0.0 1.1 %pack.1 = (bf16[8,8,8,256]{3,2,1,0:T(8,128)(2,1)S(1)}, bf16[8,16,8,256]{3,2,1,0:T(8,128)(2,1)S(1)}, f32[2,8,8,256]{3,2,1,0:T(8,128)S(1)}) custom-call(s32[2,4]{1,0:T(2,128)} %bitcast.2, s32[1]{0:T(128)} %bitcast.1.place_ref.refs_3_, bf16[64,2,4,256]{3,2,1,0:T(4,128)(2,1)} %raw_hbm.1), custom_call_target="tpu_custom_call" | custom-call | tf_op jit(solution)/shard_map/pack/pallas_call | solution.py:49
  1.1 16.0 %all_to_all.15.pieces_ref = bf16[8,16,8,256]{3,2,1,0:T(8,128)(2,1)S(1)} all-to-all(bf16[8,16,8,256]{3,2,1,0:T(8,128)(2,1)S(1)} %get-tuple-element.13), channel_id=1, replica_groups=mesh['x'=4,'zl'=2,'y'=8,'zh'=4,'c'=2] {'zl','x'}, dimensions={0} | all-to-all | bytes 1048576 | tf_op jit(solution)/shard_map/all_to_all | solution.py:222
  17.1 0.1 choose.1
  17.2 11.4 %all_to_all.16.recv_ref.refs_1_ = bf16[8,16,8,256]{3,2,1,0:T(8,128)(2,1)S(1)} all-to-all(bf16[8,16,8,256]{3,2,1,0:T(8,128)(2,1)S(1)} %choose.1), channel_id=1, replica_groups=mesh['x'=4,'zl'=2,'y'=8,'zh'=4,'c'=2] {'zl','x'}, dimensions={0} | all-to-all | bytes 1048576 | tf_op jit(solution)/shard_map/all_to_all | solution.py:223
  28.7 0.0 copy-start
  28.7 6.6 %collective-permute-start.1 = (bf16[8,2,8,256]{3,2,1,0:T(8,128)(2,1)S(1)}, bf16[8,2,8,256]{3,2,1,0:T(8,128)(2,1)S(1)}, u32[]{:S(2)}, u32[]{:S(2)}) collective-permute-start(bf16[8,2,8,256]{3,2,1,0:T(8,128)(2,1)S(1)} %get-tuple-element.17), channel_id=1, source_target_pairs={{1,2},{2,1},{3,4},{4,3},{5,6},{6,5},{7,8},{8,7},{9,10},{10,9},{11,... | collective-permute-start | bytes 196616 | tf_op jit(solution)/shard_map/ppermute | solution.py:227
  35.4 0.0 copy-done
  35.4 1.4 %shard_map.37.refs_6_ = f32[32,32,128]{2,1,0:T(8,128)S(1)} custom-call(f32[3,4,256]{2,1,0:T(4,128)S(1)} %copy-done, bf16[8,16,8,256]{3,2,1,0:T(8,128)(2,1)S(1)} %all_to_all.16.recv_ref.refs_1_, bf16[8,8,8,256]{3,2,1,0:T(8,128)(2,1)S(1)} %get-tuple-element.14.refs_2_, s32[1]{0:T(128)} %bitcast.1.place_ref.refs_3_), custom_call_target="tpu_custom_call" | custom-call | tf_op jit(solution)/shard_map/pallas_call | solution.py:181
  36.8 1.9 %collective-permute-start = (bf16[8,2,8,256]{3,2,1,0:T(8,128)(2,1)S(1)}, bf16[8,2,8,256]{3,2,1,0:T(8,128)(2,1)S(1)}, u32[]{:S(2)}, u32[]{:S(2)}) collective-permute-start(bf16[8,2,8,256]{3,2,1,0:T(8,128)(2,1)S(1)} %get-tuple-element.16), channel_id=1, source_target_pairs={{0,1},{1,0},{2,3},{3,2},{4,5},{5,4},{6,7},{7,6},{8,9},{9,8},{10,11... | collective-permute-start | bytes 196616 | tf_op jit(solution)/shard_map/ppermute | solution.py:230
  38.7 0.0 collective-permute-done.1.refs_5_
  38.8 1.2 %collective-permute-done.refs_4_ = bf16[8,2,8,256]{3,2,1,0:T(8,128)(2,1)S(1)} collective-permute-done((bf16[8,2,8,256]{3,2,1,0:T(8,128)(2,1)S(1)}, bf16[8,2,8,256]{3,2,1,0:T(8,128)(2,1)S(1)}, u32[]{:S(2)}, u32[]{:S(2)}) %collective-permute-start) | collective-permute-done | bytes 65568 | tf_op jit(solution)/shard_map/ppermute | solution.py:230
  40.0 1.5 %shard_map.39 = f32[32,32,128]{2,1,0:T(8,128)S(1)} custom-call(f32[3,4,256]{2,1,0:T(4,128)S(1)} %copy-done, bf16[8,16,8,256]{3,2,1,0:T(8,128)(2,1)S(1)} %all_to_all.16.recv_ref.refs_1_, bf16[8,8,8,256]{3,2,1,0:T(8,128)(2,1)S(1)} %get-tuple-element.14.refs_2_, s32[1]{0:T(128)} %bitcast.1.place_ref.refs_3_, ...), custom_call_target="tpu_custom_call" | custom-call | tf_op jit(solution)/shard_map/pallas_call | solution.py:181
  41.4 2.1 %collective-permute-start.2 = (f32[32,32,128]{2,1,0:T(8,128)S(1)}, f32[32,32,128]{2,1,0:T(8,128)S(1)}, u32[]{:S(2)}, u32[]{:S(2)}) collective-permute-start(f32[32,32,128]{2,1,0:T(8,128)S(1)} %shard_map.39), channel_id=1, source_target_pairs={{0,1},{1,0},{2,3},{3,2},{4,5},{5,4},{6,7},{7,6},{8,9},{9,8},{10,11... | collective-permute-start | bytes 1572872 | tf_op jit(solution)/shard_map/ppermute | solution.py:233
  43.5 2.8 %shard_map.38 = f32[32,32,128]{2,1,0:T(8,128)S(1)} custom-call(f32[3,4,256]{2,1,0:T(4,128)S(1)} %copy-done, bf16[8,16,8,256]{3,2,1,0:T(8,128)(2,1)S(1)} %all_to_all.16.recv_ref.refs_1_, bf16[8,8,8,256]{3,2,1,0:T(8,128)(2,1)S(1)} %get-tuple-element.14.refs_2_, s32[1]{0:T(128)} %bitcast.1.place_ref.refs_3_, ...), custom_call_target="tpu_custom_call" | custom-call | tf_op jit(solution)/shard_map/pallas_call | solution.py:181
  46.3 0.0 collective-permute-done.2
  46.3 0.1 add_convert_fusion
  46.4 27.5 %all_to_all.17.refs_0_ = bf16[32,32,128]{2,1,0:T(8,128)(2,1)S(1)} all-to-all(bf16[32,32,128]{2,1,0:T(8,128)(2,1)S(1)} %add_convert_fusion), channel_id=1, replica_groups=mesh['x'=4,'zl'=2,'y'=8,'zh'=4,'c'=2] {'y','zh'}, dimensions={0} | all-to-all | bytes 524288 | tf_op jit(solution)/shard_map/all_to_all | solution.py:235
  73.9 0.7 finish.1
  (1 shorter events, 0.0 us)
Async XLA Ops:
  28.7 6.7 %copy-start = (f32[3,4,256]{2,1,0:T(4,128)S(1)}, f32[3,4,256]{2,1,0:T(4,128)}, u32[]{:S(2)}) copy-start(f32[3,4,256]{2,1,0:T(4,128)} %refs_0_.5) | copy-start | bytes 36868
  28.7 10.0 %collective-permute-start.1 = (bf16[8,2,8,256]{3,2,1,0:T(8,128)(2,1)S(1)}, bf16[8,2,8,256]{3,2,1,0:T(8,128)(2,1)S(1)}, u32[]{:S(2)}, u32[]{:S(2)}) collective-permute-start(bf16[8,2,8,256]{3,2,1,0:T(8,128)(2,1)S(1)} %get-tuple-element.17), channel_id=1, source_target_pairs={{1,2},{2,1},{3,4},{4,3},{5,6},{6,5},{7,8},{8,7},{9,10},{10,9},{11,... | collective-permute-start | bytes 196616 | tf_op jit(solution)/shard_map/ppermute | solution.py:227
  36.8 3.1 %collective-permute-start = (bf16[8,2,8,256]{3,2,1,0:T(8,128)(2,1)S(1)}, bf16[8,2,8,256]{3,2,1,0:T(8,128)(2,1)S(1)}, u32[]{:S(2)}, u32[]{:S(2)}) collective-permute-start(bf16[8,2,8,256]{3,2,1,0:T(8,128)(2,1)S(1)} %get-tuple-element.16), channel_id=1, source_target_pairs={{0,1},{1,0},{2,3},{3,2},{4,5},{5,4},{6,7},{7,6},{8,9},{9,8},{10,11... | collective-permute-start | bytes 196616 | tf_op jit(solution)/shard_map/ppermute | solution.py:230
  41.4 4.8 %collective-permute-start.2 = (f32[32,32,128]{2,1,0:T(8,128)S(1)}, f32[32,32,128]{2,1,0:T(8,128)S(1)}, u32[]{:S(2)}, u32[]{:S(2)}) collective-permute-start(f32[32,32,128]{2,1,0:T(8,128)S(1)} %shard_map.39), channel_id=1, source_target_pairs={{0,1},{1,0},{2,3},{3,2},{4,5},{5,4},{6,7},{7,6},{8,9},{9,8},{10,11... | collective-permute-start | bytes 1572872 | tf_op jit(solution)/shard_map/ppermute | solution.py:233
